TPU v7x, 32 devices: a whole 2x2x4 slice. The times are simulated.
32 devices in a mesh: seq: 16 (over z, y, x), head: 2 (over core).
Axes of the slice: x: 2, y: 2, z: 4, core: 2. Of those that a mesh axis runs over, the one named last changes fastest.
Arguments:
- hidden_in: float32 [1, 2048, 1024], P(None, 'seq'), may hold values from -6 to 6
- norm_gain: float32 [1024], replicated, may hold values from 0.5 to 1.5
- proj_z: bfloat16 [1024, 2048], P(None, 'head'), may hold values from -0.1875 to 0.1875
- proj_x: bfloat16 [1024, 2048], P(None, 'head'), may hold values from -0.1875 to 0.1875
- proj_bc: bfloat16 [1024, 256], replicated, may hold values from -0.1875 to 0.1875
- proj_dt: bfloat16 [1024, 32], P(None, 'head'), may hold values from -0.1875 to 0.1875
- conv_x_weight: float32 [4, 2048], P(None, 'head'), may hold values from -3 to 3
- conv_x_bias: float32 [2048], P('head'), may hold values from -3 to 3
- conv_bc_weight: float32 [4, 256], replicated, may hold values from -3 to 3
- conv_bc_bias: float32 [256], replicated, may hold values from -3 to 3
- step_bias: float32 [32], P('head'), may hold values from -6.9 to -2.25
- log_rate: float32 [32], P('head'), may hold values from 0 to 2.77
- skip_gain: float32 [32], P('head'), may hold values from 0.5 to 1.5
- gate_gain: float32 [2048], P('head'), may hold values from 0.5 to 1.5
- proj_out: bfloat16 [2048, 1024], P('head'), may hold values from -0.125 to 0.125
- out_grad: float32 [1, 2048, 1024], P(None, 'seq'), may hold values from -6 to 6
Outputs:
- hidden_out: float32 [1, 2048, 1024], P(None, 'seq')
- grad_in: float32 [1, 2048, 1024], P(None, 'seq')
- grad_norm_gain: float32 [1024], replicated
- grad_proj_z: float32 [1024, 2048], P('seq', 'head')
- grad_proj_x: float32 [1024, 2048], P('seq', 'head')
- grad_proj_bc: float32 [1024, 256], P(('seq', 'head'))
- grad_proj_dt: float32 [1024, 32], P('seq', 'head')
- grad_conv_x_weight: float32 [4, 2048], P(None, 'head')
- grad_conv_x_bias: float32 [2048], P('head')
- grad_conv_bc_weight: float32 [4, 256], replicated
- grad_conv_bc_bias: float32 [256], replicated
- grad_step_bias: float32 [32], P('head')
- grad_log_rate: float32 [32], P('head')
- grad_skip_gain: float32 [32], P('head')
- grad_gate_gain: float32 [2048], P('head')
- grad_proj_out: float32 [2048, 1024], P('head', 'seq')
All inputs are finite; a program needn't handle non-finite values.
Results may differ from a plain program's by a relative error of at most 0.0099.
Values sent between devices are 32-bit elements; how exact they have to be, the bound alone decides.
No kernel may reach another device: no remote copies, remote signals or barrier semaphores. Data moves between devices by JAX's collectives and lax.ppermute only.
A program may use at most 192 MiB of HBM per device.

v0:
```python
import jax
import jax.numpy as jnp
from jax import lax
from jax.sharding import PartitionSpec as P

INNER = 2048
HEADDIM = 64
STATE = 128
CONV = 4


EPS = 1e-05
HIGHEST = lax.Precision.HIGHEST


def shifted(value, axis, by):
    peers = lax.axis_size(axis)
    pairs = [(i, i + by) for i in range(peers) if 0 <= i + by < peers]
    return lax.ppermute(value, axis, pairs)


def prefix(part, axis, combine, identity, reverse):
    count = lax.axis_size(axis)
    place = lax.axis_index(axis)
    ahead = count - 1 - place if reverse else place
    gathered = jax.tree.map(lambda a: lax.all_gather(a, axis), part)
    state = jax.tree.map(lambda a, e: jnp.zeros_like(a) + jnp.asarray(e, a.dtype), part, identity)

    def one(hop, state):
        source = count - 1 - hop if reverse else hop
        return combine(
            state, jax.tree.map(lambda a: lax.dynamic_index_in_dim(a, source, 0, False), gathered)
        )

    return lax.fori_loop(0, ahead, one, state)


def matmul(left, right):
    return jnp.dot(left, right, preferred_element_type=jnp.float32)


def matmul_nt(left, right):
    return lax.dot_general(
        left, right, (((1,), (1,)), ((), ())), preferred_element_type=jnp.float32
    )


def matmul_tn(left, right):
    return lax.dot_general(
        left, right, (((0,), (0,)), ((), ())), preferred_element_type=jnp.float32
    )


def round_keep(values):
    return lax.optimization_barrier(values.astype(jnp.bfloat16)).astype(jnp.float32)


def silu_slope(values):
    logistic = jax.nn.sigmoid(values)
    return logistic * (1.0 + values * (1.0 - logistic))


def causal_conv(padded, kernel, bias_vec, length):
    result = bias_vec + kernel[0] * padded[:, 0:length]
    for offset in range(1, kernel.shape[0]):
        result = result + kernel[offset] * padded[:, offset : offset + length]
    return result


def conv_back(padded, kernel, grad_out, length):
    grad_pad = jnp.zeros_like(padded)
    kernel_rows = []
    for offset in range(kernel.shape[0]):
        kernel_rows.append(jnp.sum(grad_out * padded[:, offset : offset + length], axis=(0, 1)))
        grad_pad = grad_pad.at[:, offset : offset + length].add(kernel[offset] * grad_out)
    return (grad_pad, jnp.stack(kernel_rows), jnp.sum(grad_out, axis=(0, 1)))


def ssd_out(x_heads, step_size, decay_rate, b_input, c_output, state_in):
    step_rows = jnp.transpose(step_size, (0, 2, 1))
    cumulative = jnp.cumsum(step_rows * decay_rate[None, :, None], axis=2)
    length = x_heads.shape[1]
    causal_mask = (jnp.arange(length)[:, None] >= jnp.arange(length)[None, :])[None, None, :, :]
    log_gaps = cumulative[:, :, :, None] - cumulative[:, :, None, :]
    decay_mat = jnp.where(causal_mask, jnp.exp(jnp.where(causal_mask, log_gaps, 0.0)), 0.0)
    inner_prod = jnp.einsum("stn,sun->stu", c_output, b_input, precision=HIGHEST)
    weights = inner_prod[:, None, :, :] * decay_mat * step_rows[:, :, None, :]
    local_part = jnp.einsum("shtu,suhp->sthp", weights, x_heads, precision=HIGHEST)
    carried = jnp.einsum("stn,shpn->sthp", c_output, state_in, precision=HIGHEST)
    return local_part + jnp.transpose(jnp.exp(cumulative), (0, 2, 1))[:, :, :, None] * carried


def ssd_summary(x_heads, step_size, decay_rate, b_input):
    cumulative = jnp.cumsum(step_size * decay_rate, axis=1)
    totals = cumulative[:, -1, :]
    factor = jnp.exp(totals[:, None, :] - cumulative) * step_size
    states = jnp.einsum("sth,sthp,stn->shpn", factor, x_heads, b_input, precision=HIGHEST)
    return (jnp.exp(totals), states)


def link_states(earlier, later):
    return (earlier[0] * later[0], later[0][:, :, None, None] * earlier[1] + later[1])


def norm_back(block_in, inv_rms, in_grad, block_grad, norm_gain):
    norm_hat = block_in * inv_rms
    gain_part = jnp.sum(in_grad * norm_hat, axis=(0, 1))
    hat_in = in_grad * norm_gain
    grad_block = block_grad + inv_rms * (
        hat_in - norm_hat * jnp.mean(hat_in * norm_hat, axis=-1, keepdims=True)
    )
    return (grad_block, gain_part)


def body(
    hidden_in,
    norm_gain,
    proj_z,
    proj_x,
    proj_bc,
    proj_dt,
    conv_x_weight,
    conv_x_bias,
    conv_bc_weight,
    conv_bc_bias,
    step_bias,
    log_rate,
    skip_gain,
    gate_gain,
    proj_out,
    out_grad,
):
    batch, length, width = hidden_in.shape
    heads = step_bias.shape[0]
    inner = proj_z.shape[1]
    rows = batch * length
    edge = CONV - 1
    head_index = lax.axis_index("head")
    head_count = lax.axis_size("head")
    seq_count = lax.axis_size("seq")
    inv_rms = lax.rsqrt(jnp.mean(hidden_in * hidden_in, axis=-1, keepdims=True) + EPS)
    normed = (hidden_in * inv_rms * norm_gain).astype(jnp.bfloat16)
    normed_rows = normed.reshape(rows, width)
    gate_pre = matmul(normed_rows, proj_z).reshape(batch, length, inner)
    x_pre = matmul(normed_rows, proj_x).reshape(batch, length, inner)
    bc_pre = matmul(normed_rows, proj_bc).reshape(batch, length, 2 * STATE)
    step_pre = matmul(normed_rows, proj_dt).reshape(batch, length, heads)
    edge_in = shifted(
        jnp.concatenate([x_pre[:, length - edge :], bc_pre[:, length - edge :]], axis=-1), "seq", 1
    )
    x_padded = jnp.concatenate([edge_in[:, :, :inner], x_pre], axis=1)
    bc_padded = jnp.concatenate([edge_in[:, :, inner:], bc_pre], axis=1)
    x_conv = causal_conv(x_padded, conv_x_weight, conv_x_bias, length)
    bc_conv = causal_conv(bc_padded, conv_bc_weight, conv_bc_bias, length)
    x_heads = round_keep(jax.nn.silu(x_conv)).reshape(batch, length, heads, HEADDIM)
    bc_act = round_keep(jax.nn.silu(bc_conv))
    b_input = bc_act[:, :, :STATE]
    c_output = bc_act[:, :, STATE:]
    step_size = jax.nn.softplus(step_pre + step_bias)
    decay_rate = -jnp.exp(log_rate)
    decay_total, state_local = ssd_summary(x_heads, step_size, decay_rate, b_input)
    identity = (jnp.ones_like(decay_total), jnp.zeros_like(state_local))
    _, state_in = prefix((decay_total, state_local), "seq", link_states, identity, False)
    y_heads = (
        ssd_out(x_heads, step_size, decay_rate, b_input, c_output, state_in)
        + skip_gain[:, None] * x_heads
    )
    y_flat = y_heads.reshape(batch, length, inner)
    gated = y_flat * jax.nn.silu(gate_pre)
    square_sum = lax.psum(jnp.sum(gated * gated, axis=-1, keepdims=True), "head")
    gate_rms = lax.rsqrt(square_sum / INNER + EPS)
    gate_normed = (gated * gate_rms * gate_gain).astype(jnp.bfloat16)
    gate_normed_rows = gate_normed.reshape(rows, inner)
    out_sum = lax.psum(matmul(gate_normed_rows, proj_out).reshape(batch, length, width), "head")
    hidden_out = hidden_in + out_sum
    grad_bf = out_grad.astype(jnp.bfloat16).reshape(rows, width)
    normed_grad = matmul_nt(grad_bf, proj_out).reshape(batch, length, inner)
    gate_hat = gated * gate_rms
    grad_gate_gain = jnp.sum(normed_grad * gate_hat, axis=(0, 1))
    hat_grad = normed_grad * gate_gain
    hat_dot = lax.psum(jnp.sum(hat_grad * gate_hat, axis=-1, keepdims=True), "head")
    gated_grad = gate_rms * (hat_grad - gate_hat * hat_dot / INNER)
    y_grad = (gated_grad * jax.nn.silu(gate_pre)).reshape(batch, length, heads, HEADDIM)
    gate_grad = gated_grad * y_flat * silu_slope(gate_pre)
    grad_skip_gain = jnp.sum(y_grad * x_heads, axis=(0, 1, 3))
    _, out_vjp = jax.vjp(ssd_out, x_heads, step_size, decay_rate, b_input, c_output, state_in)
    x_grad_a, step_grad_a, rate_grad_a, b_grad_a, c_grad, state_in_grad = out_vjp(y_grad)
    _, state_grad = prefix((decay_total, state_in_grad), "seq", link_states, identity, True)
    decay_grad = jnp.sum(state_in * state_grad, axis=(2, 3))
    _, sum_vjp = jax.vjp(ssd_summary, x_heads, step_size, decay_rate, b_input)
    x_grad_b, step_grad_b, rate_grad_b, b_grad_b = sum_vjp((decay_grad, state_grad))
    x_heads_grad = x_grad_a + x_grad_b + skip_gain[:, None] * y_grad
    x_conv_grad = x_heads_grad.reshape(batch, length, inner) * silu_slope(x_conv)
    bc_act_grad = lax.psum(jnp.concatenate([b_grad_a + b_grad_b, c_grad], axis=-1), "head")
    bc_conv_grad = bc_act_grad * silu_slope(bc_conv)
    step_pre_grad = (step_grad_a + step_grad_b) * jax.nn.sigmoid(step_pre + step_bias)
    grad_step_bias = jnp.sum(step_pre_grad, axis=(0, 1))
    grad_log_rate = (rate_grad_a + rate_grad_b) * decay_rate
    x_pad_grad, grad_conv_x_weight, grad_conv_x_bias = conv_back(
        x_padded, conv_x_weight, x_conv_grad, length
    )
    bc_pad_grad, grad_conv_bc_weight, grad_conv_bc_bias = conv_back(
        bc_padded, conv_bc_weight, bc_conv_grad, length
    )
    edge_grad = shifted(
        jnp.concatenate([x_pad_grad[:, :edge], bc_pad_grad[:, :edge]], axis=-1), "seq", -1
    )
    x_pre_grad = x_pad_grad[:, edge:].at[:, length - edge :].add(edge_grad[:, :, :inner])
    bc_pre_grad = bc_pad_grad[:, edge:].at[:, length - edge :].add(edge_grad[:, :, inner:])
    gate_bf = gate_grad.astype(jnp.bfloat16).reshape(rows, inner)
    x_bf = x_pre_grad.astype(jnp.bfloat16).reshape(rows, inner)
    bc_bf = bc_pre_grad.astype(jnp.bfloat16).reshape(rows, 2 * STATE)
    step_bf = step_pre_grad.astype(jnp.bfloat16).reshape(rows, heads)
    in_part = matmul_nt(gate_bf, proj_z) + matmul_nt(x_bf, proj_x) + matmul_nt(step_bf, proj_dt)
    half = width // head_count
    bc_weight_half = lax.dynamic_slice_in_dim(proj_bc, head_index * half, half, 0)
    own_cols = lax.dynamic_slice_in_dim(in_part, head_index * half, half, 1) + matmul_nt(
        bc_bf, bc_weight_half
    )
    in_part = lax.dynamic_update_slice_in_dim(in_part, own_cols, head_index * half, 1).reshape(
        batch, length, width
    )
    in_grad = lax.psum(in_part, "head")
    grad_in, grad_norm_gain = norm_back(hidden_in, inv_rms, in_grad, out_grad, norm_gain)
    quarter = width // (seq_count * head_count)
    picked = lax.dynamic_slice_in_dim(
        normed_rows.reshape(rows, seq_count, head_count, quarter), head_index, 1, 2
    ).reshape(rows, seq_count * quarter)
    row_grads = (
        lax.psum_scatter(matmul_tn(normed_rows, gate_bf), "seq", scatter_dimension=0, tiled=True),
        lax.psum_scatter(matmul_tn(normed_rows, x_bf), "seq", scatter_dimension=0, tiled=True),
        lax.psum_scatter(matmul_tn(normed_rows, step_bf), "seq", scatter_dimension=0, tiled=True),
        lax.psum_scatter(matmul_tn(picked, bc_bf), "seq", scatter_dimension=0, tiled=True),
        lax.psum_scatter(
            matmul_tn(gate_normed_rows, grad_bf), "seq", scatter_dimension=1, tiled=True
        ),
    )
    small = lax.psum(
        (
            grad_norm_gain,
            grad_conv_x_weight,
            grad_conv_x_bias,
            grad_conv_bc_weight,
            grad_conv_bc_bias,
            grad_step_bias,
            grad_log_rate,
            grad_skip_gain,
            grad_gate_gain,
        ),
        "seq",
    )
    return (
        hidden_out,
        grad_in,
        small[0],
        row_grads[0],
        row_grads[1],
        row_grads[3],
        row_grads[2],
        small[1],
        small[2],
        small[3],
        small[4],
        small[5],
        small[6],
        small[7],
        small[8],
        row_grads[4],
    )


def solution(mesh):
    placed = (
        P(None, "seq", None),
        P(),
        P(None, "head"),
        P(None, "head"),
        P(),
        P(None, "head"),
        P(None, "head"),
        P("head"),
        P(),
        P(),
        P("head"),
        P("head"),
        P("head"),
        P("head"),
        P("head", None),
        P(None, "seq", None),
    )
    return jax.shard_map(
        body,
        mesh=mesh,
        in_specs=placed,
        out_specs=(
            P(None, "seq", None),
            P(None, "seq", None),
            P(),
            P("seq", "head"),
            P("seq", "head"),
            P(("seq", "head"), None),
            P("seq", "head"),
            P(None, "head"),
            P("head"),
            P(),
            P(),
            P("head"),
            P("head"),
            P("head"),
            P("head"),
            P("head", "seq"),
        ),
        check_vma=False,
    )
```

profile of v0, /device:TPU:0, one launch (start us, length us, event | category | flops | bytes accessed | tf_op | source)
XLA Modules:
  0.0 850.5 jit_solution(28374140216089950)
XLA Ops:
  11.7 4.9 collective-permute-start
  29.6 42.0 %all_gather.18 = f32[16,1,16]{2,1,0:T(1,128)} all-gather(f32[1,1,16]{2,1,0:T(1,128)} %get-tuple-element.400), channel_id=1, replica_groups=mesh['seq'=16,'head'=2] {'seq'}, dimensions={0}, use_global_device_ids=true | all-gather | bytes 1088 | tf_op jit(solution)/shard_map/all_gather | solution.py:26
  74.7 62.7 %all-gather.5.cloned.1.call-done = f32[256,64,128]{2,1,0:T(8,128)} async-done(((f32[16,64,128]{2,1,0:T(8,128)}), f32[256,64,128]{2,1,0:T(8,128)}) %all-gather.5.cloned.1.call-update) | async-done | bytes 8388624 | tf_op jit(solution)/shard_map/all_gather | solution.py:26
  138.7 3.3 fusion.3
  144.1 2.8 multiply_reduce_fusion.12
  146.9 3.1 psum.98
  151.1 3.9 multiply_reduce_fusion.2
  155.1 3.1 psum.100
  158.1 2.2 fusion.19
  164.1 2.2 fusion.79
  169.9 3.5 fusion.15
  174.0 2.5 reduce_window_sum.55
  186.3 3.0 convolution_bitcast_fusion.2
  192.0 111.9 %all-gather.7.cloned.1.call-done = f32[256,64,128]{2,1,0:T(8,128)} async-done(((f32[16,64,128]{2,1,0:T(8,128)}), f32[256,64,128]{2,1,0:T(8,128)}) %all-gather.7.cloned.1.call-update) | async-done | bytes 8388624 | tf_op jit(solution)/shard_map/all_gather | solution.py:26
  304.0 27.7 %while.37 = (s32[]{:T(128)}, f32[1,16,64,128]{3,2,1,0:T(8,128)S(1)}, s32[]{:T(128)}, f32[16,1,16]{2,1,0:T(1,128)}, f32[16,1,16,64,128]{4,3,2,1,0:T(8,128)}, /*index=5*/s32[]{:T(128)}, s32[]{:T(128)}, s32[]{:T(128)}, s32[]{:T(128)}) while((s32[]{:T(128)}, f32[1,16,64,128]{3,2,1,0:T(8,128)S(1)}, s32[]{:T(128)}, f32[16,1,16]{2,1,0:T(1,128)}, ...), condition=%wide.region_11.12_spmd, body=%wide.region_10.11_spmd.sunk | while | flops 262150 | bytes 1573211 | solution.py:35
  338.8 2.3 fusion.105
  343.6 2.6 scatter-add.29
  348.2 2.6 scatter-add.30
  363.4 7.4 all-reduce.8.cloned.1.call-done
  375.2 4.3 collective-permute-done.1
  379.9 2.6 convolution_add_fusion.1
  385.4 3.8 fusion.41
  390.2 2.7 fusion.48
  394.2 2.7 fusion.38
  398.2 53.5 %reduce-scatter.16.cloned.1.call-done = f32[64,16]{1,0:T(8,128)} async-done(((f32[1024,16]{1,0:T(8,128)}), f32[64,16]{1,0:T(8,128)}) %reduce-scatter.16.cloned.1.call-update) | async-done | bytes 4112
  453.1 17.2 %all-reduce.10.cloned.1.call-done = (f32[1,128,1024]{2,1,0:T(8,128)}, f32[1,128,1024]{2,1,0:T(8,128)}) async-done(((f32[1,128,1024]{2,1,0:T(8,128)}, f32[1,128,1024]{2,1,0:T(8,128)}), (f32[1,128,1024]{2,1,0:T(8,128)}, f32[1,128,1024]{2,1,0:T(8,128)})) %all-reduce.10.cloned.1.call-update) | async-done | bytes 1048592 | tf_op jit(solution)/shard_map/psum | solution.py:174
  471.7 78.3 %all-reduce.3 = (f32[1024]{0:T(1024)}, f32[4,1024]{1,0:T(4,128)}, f32[1024]{0:T(1024)}, f32[4,256]{1,0:T(4,128)}, f32[256]{0:T(256)}, /*index=5*/f32[16]{0:T(128)}, f32[16]{0:T(128)}, f32[16]{0:T(128)}, f32[1024]{0:T(1024)}) all-reduce(f32[1024]{0:T(1024)S(1)} %get-tuple-element.335, ...), channel_id=1, replica_groups=mesh['seq'=16,'head'=2] {'seq'}, use_global_device_ids=true, to_apply=%region_25.26 | all-reduce | flops 8496 | bytes 67968 | tf_op jit(solution)/shard_map/psum | solution.py:238
  550.0 2.4 multiply_add_fusion
  552.3 19.5 %reduce-scatter.14.cloned.1.call-done = f32[1024,64]{0,1:T(8,128)} async-done(((f32[1024,1024]{0,1:T(8,128)}), f32[1024,64]{0,1:T(8,128)}) %reduce-scatter.14.cloned.1.call-update) | async-done | bytes 262160 | tf_op jit(solution)/shard_map/reduce_scatter | solution.py:234
  571.8 97.6 %reduce-scatter.8.cloned.1.call-done = f32[64,1024]{1,0:T(8,128)} async-done(((f32[1024,1024]{1,0:T(8,128)}), f32[64,1024]{1,0:T(8,128)}) %reduce-scatter.8.cloned.1.call-update) | async-done | bytes 262160 | tf_op jit(solution)/shard_map/reduce_scatter | solution.py:230
  669.5 80.0 %reduce-scatter.12.cloned.1.call-done = f32[32,256]{1,0:T(8,128)} async-done(((f32[512,256]{1,0:T(8,128)}), f32[32,256]{1,0:T(8,128)}) %reduce-scatter.12.cloned.1.call-update) | async-done | bytes 32784 | tf_op jit(solution)/shard_map/reduce_scatter | solution.py:233
  749.4 94.5 %reduce-scatter.10.cloned.1.call-done = f32[64,1024]{1,0:T(8,128)} async-done(((f32[1024,1024]{1,0:T(8,128)}), f32[64,1024]{1,0:T(8,128)}) %reduce-scatter.10.cloned.1.call-update) | async-done | bytes 262160 | tf_op jit(solution)/shard_map/reduce_scatter | solution.py:231
  (349 shorter events, 109.7 us)
Async XLA Ops:
  7.2 136.9 %copy-start = (bf16[1024,1024]{1,0:T(8,128)(2,1)S(1)}, bf16[1024,1024]{1,0:T(8,128)(2,1)}, u32[]{:S(2)}) copy-start(bf16[1024,1024]{1,0:T(8,128)(2,1)} %param.42) | copy-start | bytes 6291460
  7.2 130.2 %all-gather.5.cloned.1.call-start = ((), (), s32[]{:S(2)}) async-start(), calls=%async_computation.10 | async-start | bytes 8912896 | tf_op jit(solution)/shard_map/all_gather | solution.py:26
  11.7 8.6 %collective-permute-start = (f32[1,3,1280]{2,1,0:T(4,128)S(1)}, f32[1,3,1280]{2,1,0:T(4,128)S(1)}, u32[]{:S(2)}, u32[]{:S(2)}) collective-permute-start(f32[1,3,1280]{2,1,0:T(4,128)S(1)} %pad_maximum_fusion.3), channel_id=1, source_target_pairs={{0,2},{2,4},{4,6},{6,8},{8,10},{10,12},{12,14},{14,16},{16,18},{18... | collective-permute-start | bytes 46088 | tf_op jit(solution)/shard_map/ppermute | solution.py:19
  22.2 50.9 %copy-start.13 = (bf16[1,128,1024]{2,1,0:T(8,128)(2,1)}, bf16[1,128,1024]{2,1,0:T(8,128)(2,1)S(1)}, u32[]{:S(2)}) copy-start(bf16[1,128,1024]{2,1,0:T(8,128)(2,1)S(1)} %get-tuple-element.393) | copy-start | bytes 786436
  22.4 116.2 %copy-start.14 = (bf16[1,128,1024]{1,2,0:T(8,128)(2,1)}, bf16[1,128,1024]{1,2,0:T(8,128)(2,1)S(1)}, u32[]{:S(2)}) copy-start(bf16[1,128,1024]{1,2,0:T(8,128)(2,1)S(1)} %copy.159) | copy-start | bytes 786436
  24.6 279.4 %all-gather.7.cloned.1.call-start = ((), (), s32[]{:S(2)}) async-start(), calls=%async_computation.11 | async-start | bytes 8912896 | tf_op jit(solution)/shard_map/all_gather | solution.py:26
  146.9 42.5 %copy-start.5 = (f32[128,1024]{1,0:T(8,128)}, f32[128,1024]{1,0:T(8,128)S(1)}, u32[]{:S(2)}) copy-start(f32[128,1024]{1,0:T(8,128)S(1)} %get-tuple-element.390) | copy-start | bytes 1572868
  166.4 204.4 %all-reduce.8.cloned.1.call-start = ((), (), s32[]{:S(2)}) async-start(), calls=%async_computation.5 | async-start | bytes 262144 | tf_op jit(solution)/shard_map/psum | solution.py:194
  352.8 18.0 %copy-start.53 = (f32[1,3,256]{2,1,0:T(4,128)S(1)}, f32[1,3,256]{2,1,0:T(4,128)}, u32[]{:S(2)}) copy-start(f32[1,3,256]{2,1,0:T(4,128)} %copy-done.52) | copy-start | bytes 9220
  354.2 18.3 %copy-start.75 = (f32[1,256]{1,0:T(1,128)S(1)}, f32[1,256]{1,0:T(1,128)}, u32[]{:S(2)}) copy-start(f32[1,256]{1,0:T(1,128)} %copy-done.74) | copy-start | bytes 3076
  356.2 16.3 %copy-start.77 = (f32[1,256]{1,0:T(1,128)S(1)}, f32[1,256]{1,0:T(1,128)}, u32[]{:S(2)}) copy-start(f32[1,256]{1,0:T(1,128)} %copy-done.76) | copy-start | bytes 3076
  356.9 94.8 %reduce-scatter.16.cloned.1.call-start = ((), (), s32[]{:S(2)}) async-start(), calls=%async_computation.12 | async-start | bytes 557056
  357.7 15.5 %copy-start.73 = (f32[1,256]{1,0:T(1,128)S(1)}, f32[1,256]{1,0:T(1,128)}, u32[]{:S(2)}) copy-start(f32[1,256]{1,0:T(1,128)} %copy-done.72) | copy-start | bytes 3076
  362.1 17.6 %copy-start.9 = (f32[1,128,1024]{2,1,0:T(8,128)S(1)}, f32[1,128,1024]{2,1,0:T(8,128)}, u32[]{:S(2)}) copy-start(f32[1,128,1024]{2,1,0:T(8,128)} %slice_add_fusion) | copy-start | bytes 1572868
  363.2 107.2 %all-reduce.10.cloned.1.call-start = ((), (), s32[]{:S(2)}) async-start(), calls=%async_computation.13 | async-start | bytes 2097152 | tf_op jit(solution)/shard_map/psum | solution.py:174
  373.9 5.7 collective-permute-start.1
  385.3 186.5 %reduce-scatter.14.cloned.1.call-start = ((), (), s32[]{:S(2)}) async-start(), calls=%async_computation.9 | async-start | bytes 4456448 | tf_op jit(solution)/shard_map/reduce_scatter | solution.py:234
  389.3 280.2 %reduce-scatter.8.cloned.1.call-start = ((), (), s32[]{:S(2)}) async-start(), calls=%async_computation.6 | async-start | bytes 4456448 | tf_op jit(solution)/shard_map/reduce_scatter | solution.py:230
  392.9 356.6 %reduce-scatter.12.cloned.1.call-start = ((), (), s32[]{:S(2)}) async-start(), calls=%async_computation.8 | async-start | bytes 557056 | tf_op jit(solution)/shard_map/reduce_scatter | solution.py:233
  394.2 449.8 %reduce-scatter.10.cloned.1.call-start = ((), (), s32[]{:S(2)}) async-start(), calls=%async_computation.7 | async-start | bytes 4456448 | tf_op jit(solution)/shard_map/reduce_scatter | solution.py:231
  397.0 56.1 %copy-start.86 = (f32[256]{0:T(256)S(1)}, f32[256]{0:T(256)}, u32[]{:S(2)}) copy-start(f32[256]{0:T(256)} %get-tuple-element.346) | copy-start | bytes 3076
  397.0 56.1 %copy-start.87 = (f32[256]{0:T(256)S(1)}, f32[256]{0:T(256)}, u32[]{:S(2)}) copy-start(f32[256]{0:T(256)} %get-tuple-element.347) | copy-start | bytes 3076
  397.0 56.1 %copy-start.88 = (f32[256]{0:T(256)S(1)}, f32[256]{0:T(256)}, u32[]{:S(2)}) copy-start(f32[256]{0:T(256)} %get-tuple-element.348) | copy-start | bytes 3076
  397.0 56.1 %copy-start.89 = (f32[256]{0:T(256)S(1)}, f32[256]{0:T(256)}, u32[]{:S(2)}) copy-start(f32[256]{0:T(256)} %get-tuple-element.349) | copy-start | bytes 3076
  397.1 73.3 %copy-start.8 = (f32[1,128,1024]{2,1,0:T(8,128)S(1)}, f32[1,128,1024]{2,1,0:T(8,128)}, u32[]{:S(2)}) copy-start(f32[1,128,1024]{2,1,0:T(8,128)} %param.40) | copy-start | bytes 1572868
  397.1 73.3 %copy-start.43 = (f32[1024]{0:T(1024)S(1)}, f32[1024]{0:T(1024)}, u32[]{:S(2)}) copy-start(f32[1024]{0:T(1024)} %param.41) | copy-start | bytes 12292
  397.1 73.3 %copy-start.81 = (f32[128]{0:T(128)S(1)}, f32[128]{0:T(128)}, u32[]{:S(2)}) copy-start(f32[128]{0:T(128)} %copy-done.80) | copy-start | bytes 1540
  397.1 74.5 %copy-start.58 = (f32[1024]{0:T(1024)S(1)}, f32[1024]{0:T(1024)}, u32[]{:S(2)}) copy-start(f32[1024]{0:T(1024)} %get-tuple-element.337) | copy-start | bytes 12292
  397.1 74.5 %copy-start.66 = (f32[1024]{0:T(1024)S(1)}, f32[1024]{0:T(1024)}, u32[]{:S(2)}) copy-start(f32[1024]{0:T(1024)} %get-tuple-element.333) | copy-start | bytes 12292
  397.1 74.5 %copy-start.85 = (f32[256]{0:T(256)S(1)}, f32[256]{0:T(256)}, u32[]{:S(2)}) copy-start(f32[256]{0:T(256)} %get-tuple-element.345) | copy-start | bytes 3076
  397.1 74.5 %copy-start.91 = (f32[16]{0:T(128)S(1)}, f32[16]{0:T(128)}, u32[]{:S(2)}) copy-start(f32[16]{0:T(128)} %get-tuple-element.383) | copy-start | bytes 196
  397.1 152.8 %copy-start.11 = (f32[1,128,1024]{2,1,0:T(8,128)S(1)}, f32[1,128,1024]{2,1,0:T(8,128)}, u32[]{:S(2)}) copy-start(f32[1,128,1024]{2,1,0:T(8,128)} %param.55) | copy-start | bytes 1572868
  (78 other events, 296.0 us)
Sparse Core Ops, SparseCore 0:
  24.7 112.6 all-gather.4
  166.5 137.4 all-gather.6
  357.0 13.7 all-reduce.7
  372.9 78.7 reduce-scatter.15
  454.5 15.8 all-reduce.9
  473.1 98.7 reduce-scatter.13
  574.7 94.7 reduce-scatter.7
  672.3 77.1 reduce-scatter.11
  752.3 91.6 reduce-scatter.9
where the time goes:
time: 854 us; the launch traced here: 850 us
  waiting for transfers between devices  549 us (64%)
  blocking collectives  126 us (15%)
  matrix products  54.3 us (6%)
  other arithmetic  52.3 us (6%)
  local copies, waits for them, and re-layouts  46.1 us (5%)
  between operations  15.2 us (2%)
    all_gather x2, waiting for transfers between devices, prefix(): gathered = jax.tree.map(lambda a: lax.all_gather(a, axis), part)  175 us
    reduce_scatter x1, waiting for transfers between devices, body(): lax.psum_scatter(matmul_tn(normed_rows, gate_bf), 'seq', scatter_dimensio...  97.6 us
    reduce_scatter x1, waiting for transfers between devices, body(): lax.psum_scatter(matmul_tn(normed_rows, x_bf), 'seq', scatter_dimension=0...  94.5 us
    reduce_scatter x1, waiting for transfers between devices, body(): lax.psum_scatter(matmul_tn(picked, bc_bf), 'seq', scatter_dimension=0, ti...  80 us
    psum x1, blocking collectives, body(): lax.psum((grad_norm_gain, grad_conv_x_weight, grad_conv_x_bias, grad_conv...  78.3 us
    unnamed x10, waiting for transfers between devices  53.6 us
    all_gather x1, blocking collectives, prefix(): gathered = jax.tree.map(lambda a: lax.all_gather(a, axis), part)  42 us
    reduce_scatter x1, waiting for transfers between devices, body(): lax.psum_scatter(matmul_tn(gate_normed_rows, grad_bf), 'seq', scatter_dim...  19.5 us
  transfers between devices with their start and end apart: 11, of which 10 were waited for; matrix products, arithmetic and copies ran while one was open for 8% of the time, Pallas kernels for 0%

commit v1 on v0

v1 whole, which is shorter than its diff:
```python
import functools

import jax
import jax.numpy as jnp
from jax import lax
from jax.experimental import pallas as pl
from jax.experimental.pallas import tpu as pltpu
from jax.sharding import PartitionSpec as P

INNER = 2048
HEADDIM = 64
STATE = 128
CONV = 4
EDGE = 8
LANES = 128

EPS = 1e-05
HIGHEST = lax.Precision.HIGHEST
F32 = jnp.float32
BF16 = jnp.bfloat16

NN = (((1,), (0,)), ((), ()))
NT = (((1,), (1,)), ((), ()))
TN = (((0,), (0,)), ((), ()))


def dot(left, right, dims=NN, precision=None):
    return lax.dot_general(left, right, dims, precision=precision, preferred_element_type=F32)


def call(body, outs, *args, smem=(), scratch=(), name=None, flops=0):
    moved = sum(a.size * a.dtype.itemsize for a in args)
    moved += sum(o.size * o.dtype.itemsize for o in outs)
    ins = len(args) - len(smem)
    buffers = [pltpu.VMEM(a.shape, a.dtype) for i, a in enumerate(args) if i not in smem]
    buffers += [pltpu.VMEM(o.shape, o.dtype) for o in outs]
    count = len(buffers)

    def kernel(*refs):
        given, results = refs[: len(args)], refs[len(args) : len(args) + len(outs)]
        rest = refs[len(args) + len(outs) :]
        held, sems, own = rest[:count], rest[count], rest[count + 1 :]
        sources = [r for i, r in enumerate(given) if i not in smem]
        loads = [
            pltpu.make_async_copy(r, held[k], sems.at[k]) for k, r in enumerate(sources)
        ]
        for copy in loads:
            copy.start()
        for copy in loads:
            copy.wait()
        body(*[r for i, r in enumerate(given) if i in smem], *held, *own)
        stores = [
            pltpu.make_async_copy(held[ins + k], r, sems.at[ins + k]) for k, r in enumerate(results)
        ]
        for copy in stores:
            copy.start()
        for copy in stores:
            copy.wait()

    anywhere = pl.BlockSpec(memory_space=pl.ANY)
    specs = [pl.BlockSpec(memory_space=pltpu.SMEM) if i in smem else anywhere for i in range(len(args))]
    grant = 62 * 1024 * 1024
    return pl.pallas_call(
        kernel,
        out_shape=tuple(outs),
        in_specs=specs,
        out_specs=tuple(anywhere for _ in outs),
        scratch_shapes=buffers + [pltpu.SemaphoreType.DMA((count,))] + list(scratch),
        name=name,
        compiler_params=pltpu.CompilerParams(vmem_limit_bytes=grant),
        cost_estimate=pl.CostEstimate(flops=flops, bytes_accessed=moved, transcendentals=0),
    )(*args)


def f32(*shape):
    return jax.ShapeDtypeStruct(shape, F32)


def bf16(*shape):
    return jax.ShapeDtypeStruct(shape, BF16)


def sigmoid(values):
    return 1.0 / (1.0 + jnp.exp(-values))


def silu_slope(values):
    logistic = sigmoid(values)
    return logistic * (1.0 + values * (1.0 - logistic))


def split3(values):
    high = values.astype(BF16)
    rest = values - high.astype(F32)
    mid = rest.astype(BF16)
    low = (rest - mid.astype(F32)).astype(BF16)
    return high, mid, low


def expand(values, spread):
    return dot(jnp.concatenate(split3(values), axis=1), spread)


def head_sums(values, onehot):
    high, mid, low = split3(values)
    return dot(high, onehot, NT) + dot(mid, onehot, NT) + dot(low, onehot, NT)


def row_ids(rows, cols):
    return lax.broadcasted_iota(jnp.int32, (rows, cols), 0)


def col_ids(rows, cols):
    return lax.broadcasted_iota(jnp.int32, (rows, cols), 1)


def left_kernel(ids, hid, gain, og, normed, nfull, nsend_a, nsend_b, gfull, gsend_a, gsend_b, ntr, gtr, tmp):
    n = ids.shape[0]
    h = hid[...]
    inv = lax.rsqrt(jnp.mean(h * h, axis=-1, keepdims=True) + EPS)
    nb = (h * inv * gain[...]).astype(BF16)
    normed[...] = nb
    rows = h.shape[1] // n
    quarter = h.shape[1] // 4
    for src, full, send_a, send_b, tr in (
        (nb, nfull, nsend_a, nsend_b, ntr),
        (og[...].astype(BF16), gfull, gsend_a, gsend_b, gtr),
    ):
        tr[...] = src.astype(F32).T
        for p in range(n):
            c = ids[p]
            tmp[p * rows : (p + 1) * rows, :] = tr[pl.ds(pl.multiple_of(c * rows, rows), rows), :]
        full[...] = tmp[...].astype(BF16)
        send_a[...] = tmp[2 * quarter :, :]
        send_b[0:quarter, :] = tmp[quarter : 2 * quarter, :]
        send_b[quarter:, :] = tmp[3 * quarter :, :]


def front_kernel(
    hid, edge, gain, wx, wbc, wdt, cxw, cxb, cbw, cbb, sbias, lrate, spread, eye,
    inv_o, xpad, xconv, xact, bcpad, bcconv, bcact, upre, dts, cums, cumst, dtst, etot, sloc, factor_o, xw_o,
    nb_s,
):
    length = hid.shape[0]
    heads = sbias.shape[1]
    h = hid[...]
    inv = lax.rsqrt(jnp.mean(h * h, axis=-1, keepdims=True) + EPS)
    inv_o[...] = inv
    nb_s[EDGE:, :] = h * inv * gain[...]
    e = edge[...]
    einv = lax.rsqrt(jnp.mean(e * e, axis=-1, keepdims=True) + EPS)
    nb_s[0:EDGE, :] = e * einv * gain[...]
    nb = nb_s[...].astype(BF16)
    u = dot(nb, wdt[...])[EDGE:, :] + sbias[...]
    upre[...] = u
    dt = jnp.maximum(u, 0.0) + jnp.log1p(jnp.exp(-jnp.abs(u)))
    dts[...] = dt
    rate = -jnp.exp(lrate[...])
    lower = (row_ids(length, length) >= col_ids(length, length)).astype(F32)
    cum = dot(lower, dt * rate, precision=HIGHEST)
    cums[...] = cum
    cumst[...] = dot(eye[...], cum, NT, precision=HIGHEST)
    dtst[...] = dot(eye[...], dt, NT, precision=HIGHEST)
    tot = cum[length - 1 :, :]
    etot[...] = jnp.zeros_like(etot)
    etot[:, 0:heads] = jnp.exp(tot)
    factor = jnp.exp(tot - cum) * dt
    fac = expand(factor, spread[...])
    factor_o[...] = fac
    bcpad[...] = dot(nb, wbc[...])
    conv = cbb[...] + cbw[0:1, :] * bcpad[EDGE - 3 : EDGE - 3 + length, :]
    for k in range(1, CONV):
        conv = conv + cbw[k : k + 1, :] * bcpad[EDGE - 3 + k : EDGE - 3 + k + length, :]
    bcconv[...] = conv
    bca = (conv * sigmoid(conv)).astype(BF16)
    bcact[...] = bca
    b = bca[:, 0:STATE]
    tile = 256
    for j in range(wx.shape[1] // tile):
        cols = slice(j * tile, (j + 1) * tile)
        xpad[:, cols] = dot(nb, wx[:, cols])
        conv = cxb[:, cols] + cxw[0:1, cols] * xpad[EDGE - 3 : EDGE - 3 + length, cols]
        for k in range(1, CONV):
            conv = conv + cxw[k : k + 1, cols] * xpad[EDGE - 3 + k : EDGE - 3 + k + length, cols]
        xconv[:, cols] = conv
        xb = (conv * sigmoid(conv)).astype(BF16)
        xact[:, cols] = xb
        xw = (fac[:, cols] * xb.astype(F32)).astype(BF16)
        xw_o[:, cols] = xw
        sloc[:, cols] = dot(b, xw, TN)


def scan_kernel(reverse, part, etot, spread, out, dec_s):
    n = part.shape[0]
    heads = spread.shape[0] // 3
    dec_s[...] = expand(etot[...][:, 0:heads], spread[...])

    def one(step, state):
        j = n - 1 - step if reverse else step
        out[j] = state
        return dec_s[pl.ds(j, 1), :] * state + part[j]

    lax.fori_loop(0, n, one, jnp.zeros(part.shape[1:], F32))


def local_kernel(normed, wz, gbf, wout, bcact, xact, cums, cumst, dtst, gate_pre, ngrad, yloc, mats, decs):
    length = normed.shape[0]
    gate_pre[...] = dot(normed[...], wz[...])
    bca = bcact[...]
    b, c = bca[:, 0:STATE], bca[:, STATE:]
    cb = dot(c, b, NT)
    mask = row_ids(length, length) >= col_ids(length, length)
    lane = col_ids(length, LANES)
    for j in range(xact.shape[1] // LANES):
        xp = xact[:, j * LANES : (j + 1) * LANES]
        y = None
        for half in range(2):
            head = 2 * j + half
            gap = cums[:, head : head + 1] - cumst[head : head + 1, :]
            dec = jnp.where(mask, jnp.exp(jnp.where(mask, gap, 0.0)), 0.0) * dtst[head : head + 1, :]
            m = (cb * dec).astype(BF16)
            decs[head] = dec.astype(BF16)
            mats[head] = m
            xh = jnp.where((lane < HEADDIM) == (half == 0), xp, jnp.zeros_like(xp))
            part = dot(m, xh)
            y = part if y is None else y + part
        yloc[:, j * LANES : (j + 1) * LANES] = y
    ngrad[...] = dot(gbf[...].astype(BF16), wout[...], NT)


def gate_kernel(sin, yloc, xact, bcact, cums, spread, skip, gate_pre, ngrad, ggain, yns, gated, ecum, sums):
    c = bcact[...][:, STATE:]
    ec = expand(jnp.exp(cums[...]), spread[...])
    ecum[...] = ec
    y0 = yloc[...] + ec * dot(c, sin[...].astype(BF16))
    yns[...] = y0
    gp = gate_pre[...]
    g = (y0 + skip[...] * xact[...].astype(F32)) * (gp * sigmoid(gp))
    gated[...] = g
    s1 = jnp.sum(g * g, axis=-1, keepdims=True)
    s2 = jnp.sum(ngrad[...] * ggain[...] * g, axis=-1, keepdims=True)
    lane = col_ids(g.shape[0], LANES)
    sums[...] = jnp.where(lane == 0, s1, jnp.where(lane == 1, s2, 0.0))


def turn_kernel(
    sums, other, gated, ngrad, ggain, gate_pre, yns, xact, skip, ecum, bcact,
    dsin, ygrad, dyc, gn, gn_a, gn_b, gg, gg_a, gg_b, ggg, skp,
):
    both = sums[...] + other[...]
    rms = lax.rsqrt(both[:, 0:1] / INNER + EPS)
    hat_dot = rms * both[:, 1:2]
    g = gated[...]
    hat = g * rms
    ng = ngrad[...]
    ggg[...] = jnp.sum(ng * hat, axis=0, keepdims=True)
    gate_normed = (hat * ggain[...]).astype(BF16)
    gn[...] = gate_normed
    mid = gate_normed.shape[1] // 2
    gn_a[...] = gate_normed[:, :mid].astype(F32)
    gn_b[...] = gate_normed[:, mid:].astype(F32)
    d = rms * (ng * ggain[...] - hat * hat_dot / INNER)
    gp = gate_pre[...]
    sg = sigmoid(gp)
    yg = d * (gp * sg)
    ygrad[...] = yg
    x = xact[...].astype(F32)
    skp[...] = jnp.sum(yg * x, axis=0, keepdims=True)
    dy = (yg * ecum[...]).astype(BF16)
    dyc[...] = dy
    dsin[...] = dot(bcact[...][:, STATE:], dy, TN)
    gate_grad = (d * (yns[...] + skip[...] * x) * (sg * (1.0 + gp * (1.0 - sg)))).astype(BF16)
    gg[...] = gate_grad
    gg_a[...] = gate_grad[:, :mid].astype(F32)
    gg_b[...] = gate_grad[:, mid:].astype(F32)


def back_kernel(mats, decs, ygrad, xact, bcact, dyc, sin, yns, onehot, dxloc, bc_part, diff, kloc_o):
    length = xact.shape[0]
    lane = col_ids(length, LANES)
    dcb = jnp.zeros((length, length), F32)
    for j in range(xact.shape[1] // LANES):
        cols = slice(j * LANES, (j + 1) * LANES)
        xp = xact[:, cols]
        dyp = ygrad[:, cols].astype(BF16)
        dx = None
        for half in range(2):
            head = 2 * j + half
            dyh = jnp.where((lane < HEADDIM) == (half == 0), dyp, jnp.zeros_like(dyp))
            dcb = dcb + dot(dyh, xp, NT) * decs[head].astype(F32)
            part = dot(mats[head], dyh, TN)
            dx = part if dx is None else dx + part
        dxloc[:, cols] = dx
    bca = bcact[...]
    b, c = bca[:, 0:STATE], bca[:, STATE:]
    dcbb = dcb.astype(BF16)
    bc_part[:, 0:STATE] = dot(dcbb, c, TN)
    bc_part[:, STATE:] = dot(dcbb, b) + dot(dyc[...], sin[...].astype(BF16), NT)
    rows = head_sums(ygrad[...].astype(BF16).astype(F32) * yns[...], onehot[...])
    kloc = head_sums(xact[...].astype(F32) * dxloc[...], onehot[...])
    diff[...] = rows - kloc
    kloc_o[...] = kloc


def end_kernel(
    ds, sin, bcact, factor, xw, xact, dxloc, ygrad, skip, xconv, bc_part, diff, kloc_i, upre, dts, lrate, etot,
    onehot, skp, xcg, bcg, dstep, smalls,
):
    length = xact.shape[0]
    heads = upre.shape[1]
    dsb = ds[...].astype(BF16)
    dxst = factor[...] * dot(bcact[...][:, 0:STATE], dsb)
    bcg[:, 0:STATE] = bc_part[:, 0:STATE] + dot(xw[...], dsb, NT)
    bcg[:, STATE:] = bc_part[:, STATE:]
    x = xact[...].astype(F32)
    grad = dxloc[...] + dxst + skip[...] * ygrad[...]
    xcg[...] = grad * silu_slope(xconv[...])
    kst = head_sums(x * dxst, onehot[...])
    carry = jnp.sum(sin[...] * ds[...], axis=0, keepdims=True)
    stack = jnp.concatenate([carry, skp[...], jnp.zeros((6, carry.shape[1]), F32)], axis=0)
    sums = head_sums(stack, onehot[...])
    dec = sums[0:1, :] * etot[...][:, 0:heads]
    upper = (col_ids(length, length) >= row_ids(length, length)).astype(F32)
    below = (col_ids(length, length) < row_ids(length, length)).astype(F32)
    q = (
        dot(upper, diff[...], precision=HIGHEST)
        + dot(below, kst, precision=HIGHEST)
        + dec
    )
    rate = -jnp.exp(lrate[...])
    u = upre[...]
    dt = dts[...]
    sg = sigmoid(u)
    step = rate * q * sg + (kloc_i[...] + kst) * (sg / jnp.maximum(dt, 1e-37))
    dstep[...] = step
    smalls[...] = jnp.zeros_like(smalls)
    smalls[0:1, 0:heads] = jnp.sum(step, axis=0, keepdims=True)
    smalls[1:2, 0:heads] = jnp.sum(dt * q, axis=0, keepdims=True) * rate
    smalls[2:3, 0:heads] = sums[1:2, :]


def conv_back_rows(grad, pad, weight, wide, length):
    taps = [
        jnp.sum(grad * pad[EDGE - 3 + k : EDGE - 3 + k + length, :], axis=0, keepdims=True)
        for k in range(CONV)
    ]
    back = weight[3:4, :] * grad
    for k in range(CONV - 1):
        back = back + weight[k : k + 1, :] * wide[3 - k : 3 - k + length, :]
    return back, jnp.concatenate(taps + [jnp.sum(grad, axis=0, keepdims=True)], axis=0)


def xback_kernel(xcg, nxt, xpad, cxw, xb, xb_a, xb_b, taps, wide):
    length = xcg.shape[0]
    wide[0:length, :] = xcg[...]
    wide[length:, :] = nxt[...]
    back, small = conv_back_rows(xcg[...], xpad, cxw[...], wide, length)
    rounded = back.astype(BF16)
    xb[...] = rounded
    mid = rounded.shape[1] // 2
    xb_a[...] = rounded[:, :mid].astype(F32)
    xb_b[...] = rounded[:, mid:].astype(F32)
    taps[0 : CONV + 1, :] = small
    taps[CONV + 1 :, :] = jnp.zeros((8 - CONV - 1, small.shape[1]), F32)


def bcsum_kernel(mine, other, bcconv, out):
    out[...] = (mine[...] + other[...]) * silu_slope(bcconv[...])


def bcback_kernel(bcg, nxt, bcpad, cbw, dstep, normed, bcb, taps, dtg, bcgrad, wide):
    length = bcg.shape[0]
    wide[0:length, :] = bcg[...]
    wide[length:, :] = nxt[...]
    back, small = conv_back_rows(bcg[...], bcpad, cbw[...], wide, length)
    rounded = back.astype(BF16)
    bcb[...] = rounded
    taps[0 : CONV + 1, :] = small
    taps[CONV + 1 :, :] = jnp.zeros((8 - CONV - 1, small.shape[1]), F32)
    nb = normed[...]
    dtg[...] = dot(dstep[...].astype(BF16), nb, TN)
    bcgrad[...] = dot(nb, rounded, TN)


def product_kernel(left, recv_la, recv_lb, right, recv_ra, recv_rb, keep, send_a, send_b):
    quarter = left.shape[0] // 4
    mid = right.shape[1] // 2
    la = jnp.concatenate([left[0 : 2 * quarter, :], recv_la[...].astype(BF16)], axis=1)
    ra = jnp.concatenate([right[:, :mid], recv_ra[...].astype(BF16)], axis=0)
    keep[:, :mid] = dot(la[:quarter], ra)
    send_a[...] = dot(la[quarter:], ra)
    lb = jnp.concatenate([left[0:quarter, :], left[2 * quarter : 3 * quarter, :]], axis=0)
    lb = jnp.concatenate([lb, recv_lb[...].astype(BF16)], axis=1)
    rb = jnp.concatenate([right[:, mid:], recv_rb[...].astype(BF16)], axis=0)
    keep[:, mid:] = dot(lb[:quarter], rb)
    send_b[...] = dot(lb[quarter:], rb)


def in_kernel(gg, wz, xb, wx, dstep, wdt, bcb, wbc, first, out):
    total = dot(gg[...], wz[...], NT) + dot(xb[...], wx[...], NT)
    total = total + dot(dstep[...].astype(BF16), wdt[...], NT)
    out[...] = total + first[...] * dot(bcb[...], wbc[...], NT)


def final_kernel(mine, other, hid, inv, gain, og, grad_in, gain_grad):
    grad = mine[...] + other[...]
    scale = inv[...]
    hat = hid[...] * scale
    gain_grad[...] = jnp.sum(grad * hat, axis=0, keepdims=True)
    hat_in = grad * gain[...]
    grad_in[...] = og[...] + scale * (hat_in - hat * jnp.mean(hat_in * hat, axis=-1, keepdims=True))


def out_kernel(gn, wout, out):
    out[...] = dot(gn[...], wout[...])


def partner(value, bit):
    peers = lax.axis_size("seq")
    return lax.ppermute(value, "seq", [(i, i ^ bit) for i in range(peers)])


def shifted(value, by):
    peers = lax.axis_size("seq")
    return lax.ppermute(value, "seq", [(i, i + by) for i in range(peers) if 0 <= i + by < peers])


def other_head(value):
    return lax.ppermute(value, "head", [(0, 1), (1, 0)])


def exchange(value):
    return lax.all_to_all(value, "seq", 0, 0, tiled=True)


def weight_grad(left, right, right_a, right_b):
    full, recv_la, recv_lb = left
    rows = full.shape[0]
    cols = right.shape[1]
    recv_ra, recv_rb = partner(right_a, 1), partner(right_b, 2)
    keep, send_a, send_b = call(
        product_kernel,
        [f32(rows // 4, cols), f32(rows // 4, cols // 2), f32(rows // 4, cols // 2)],
        full, recv_la, recv_lb, right, recv_ra, recv_rb,
        name="product", flops=4 * rows * cols * right.shape[0],
    )
    got_a, got_b = partner(send_a, 2), partner(send_b, 1)
    total = keep + jnp.concatenate([got_a, got_b], axis=1)
    bit = 4
    while bit < lax.axis_size("seq"):
        half = total.shape[0] // 2
        total = total[:half] + partner(total[half:], bit)
        bit *= 2
    return total


def body(
    hidden_in, norm_gain, proj_z, proj_x, proj_bc, proj_dt, conv_x_weight, conv_x_bias, conv_bc_weight,
    conv_bc_bias, step_bias, log_rate, skip_gain, gate_gain, proj_out, out_grad,
):
    batch, length, width = hidden_in.shape
    heads = step_bias.shape[0]
    inner = proj_z.shape[1]
    n = lax.axis_size("seq")
    place = lax.axis_index("seq")
    side = lax.axis_index("head")
    bits = n.bit_length() - 1
    hid = hidden_in.reshape(length, width)
    og = out_grad.reshape(length, width)
    gain = norm_gain.reshape(1, width)
    ggain = gate_gain.reshape(1, inner)
    sbias = step_bias.reshape(1, heads)
    lrate = log_rate.reshape(1, heads)
    skip = jnp.repeat(skip_gain, HEADDIM).reshape(1, inner)
    onehot = (jnp.arange(inner)[None, :] // HEADDIM == jnp.arange(heads)[:, None]).astype(BF16)
    spread = jnp.concatenate([onehot] * 3, axis=0)
    eye = jnp.eye(heads, dtype=F32)

    edge = shifted(hid[length - EDGE :], 1)

    order = [sum(((p >> (bits - 1 - b)) & 1) << b for b in range(bits)) for p in range(n)]
    ids = jnp.array(order, jnp.int32) ^ place
    normed, nfull, nsend_a, nsend_b, gfull, gsend_a, gsend_b = call(
        left_kernel,
        [bf16(length, width)] + [bf16(width, length), f32(width // 2, length), f32(width // 2, length)] * 2,
        ids, hid, gain, og,
        smem=(0,), scratch=[pltpu.VMEM((width, length), F32)] * 3, name="left",
    )
    nleft = (nfull, partner(nsend_a, 1), partner(nsend_b, 2))
    gleft = (gfull, partner(gsend_a, 1), partner(gsend_b, 2))

    (inv, xpad, xconv, xact, bcpad, bcconv, bcact, upre, dts, cums, cumst, dtst, etot, sloc, factor, xw) = call(
        front_kernel,
        [
            f32(length, 1), f32(length + EDGE, inner), f32(length, inner), bf16(length, inner),
            f32(length + EDGE, 2 * STATE), f32(length, 2 * STATE), bf16(length, 2 * STATE),
            f32(length, heads), f32(length, heads), f32(length, heads), f32(heads, length), f32(heads, length),
            f32(1, LANES), f32(STATE, inner), f32(length, inner), bf16(length, inner),
        ],
        hid, edge, gain, proj_x, proj_bc, proj_dt, conv_x_weight, conv_x_bias.reshape(1, inner),
        conv_bc_weight, conv_bc_bias.reshape(1, 2 * STATE), sbias, lrate, spread, eye,
        scratch=[pltpu.VMEM((length + EDGE, width), F32)], name="front",
        flops=2 * length * width * (inner + 2 * STATE),
    )
    etots = exchange(jnp.broadcast_to(etot.reshape(1, 1, LANES), (n, 1, LANES))).reshape(n, LANES)

    def prefix(states, reverse):
        parts = exchange(states.reshape(n, STATE // n, inner))
        (scanned,) = call(
            functools.partial(scan_kernel, reverse), [f32(n, STATE // n, inner)], parts, etots, spread,
            scratch=[pltpu.VMEM((n, inner), F32)], name="scan",
        )
        return exchange(scanned).reshape(STATE, inner)

    sin = prefix(sloc, False)
    gate_pre, ngrad, yloc, mats, decs = call(
        local_kernel,
        [f32(length, inner)] * 3 + [bf16(heads, length, length)] * 2,
        normed, proj_z, og, proj_out, bcact, xact, cums, cumst, dtst,
        name="local", flops=6 * length * width * inner,
    )
    yns, gated, ecum, sums = call(
        gate_kernel, [f32(length, inner)] * 3 + [f32(length, LANES)],
        sin, yloc, xact, bcact, cums, spread, skip, gate_pre, ngrad, ggain, name="gate",
    )
    half = inner // 2
    dsin, ygrad, dyc, gn, gn_a, gn_b, gg, gg_a, gg_b, ggg, skp = call(
        turn_kernel,
        [f32(STATE, inner), f32(length, inner), bf16(length, inner)]
        + [bf16(length, inner), f32(length, half), f32(length, half)] * 2
        + [f32(1, inner)] * 2,
        sums, other_head(sums), gated, ngrad, ggain, gate_pre, yns, xact, skip, ecum, bcact, name="turn",
    )
    ds = prefix(dsin, True)
    dxloc, bc_part, diff, kloc = call(
        back_kernel,
        [f32(length, inner), f32(length, 2 * STATE), f32(length, heads), f32(length, heads)],
        mats, decs, ygrad, xact, bcact, dyc, sin, yns, onehot, name="back", flops=6 * length * length * inner,
    )
    (out_part,) = call(out_kernel, [f32(length, width)], gn, proj_out, name="out", flops=2 * length * width * inner)
    hidden_out = hid + (out_part + other_head(out_part))
    grad_out_t = weight_grad(gleft, gn, gn_a, gn_b)
    grad_z = weight_grad(nleft, gg, gg_a, gg_b)

    xcg, bc_grad, dstep, smalls = call(
        end_kernel,
        [f32(length, inner), f32(length, 2 * STATE), f32(length, heads), f32(8, LANES)],
        ds, sin, bcact, factor, xw, xact, dxloc, ygrad, skip, xconv, bc_part, diff, kloc, upre, dts, lrate, etot,
        onehot, skp, name="end",
    )
    (bcg,) = call(bcsum_kernel, [f32(length, 2 * STATE)], bc_grad, other_head(bc_grad), bcconv, name="bcsum")
    xb, xb_a, xb_b, xtaps = call(
        xback_kernel,
        [bf16(length, inner), f32(length, half), f32(length, half), f32(8, inner)],
        xcg, shifted(xcg[:EDGE], -1), xpad, conv_x_weight,
        scratch=[pltpu.VMEM((length + EDGE, inner), F32)], name="xback",
    )
    grad_x = weight_grad(nleft, xb, xb_a, xb_b)
    bcb, bctaps, dtg, bcgrad = call(
        bcback_kernel,
        [bf16(length, 2 * STATE), f32(8, 2 * STATE), f32(heads, width), f32(width, 2 * STATE)],
        bcg, shifted(bcg[:EDGE], -1), bcpad, conv_bc_weight, dstep, normed,
        scratch=[pltpu.VMEM((length + EDGE, 2 * STATE), F32)], name="bcback",
    )
    first = (side == 0).astype(F32).reshape(1, 1)
    (in_part,) = call(
        in_kernel, [f32(length, width)], gg, proj_z, xb, proj_x, dstep, proj_dt, bcb, proj_bc, first,
        name="in", flops=4 * length * width * inner,
    )
    grad_in, gain_grad = call(
        final_kernel, [f32(length, width), f32(1, width)], in_part, other_head(in_part), hid, inv, gain, og,
        name="final",
    )

    rows = width // n
    bc_rows = lax.dynamic_index_in_dim(bcgrad.reshape(n, 2, rows // 2, 2 * STATE), side, 1, False)
    grad_bc = jnp.sum(exchange(bc_rows), axis=0)
    dt_rows = jnp.transpose(dtg.reshape(heads, n, rows), (1, 0, 2)).reshape(n, heads * rows)
    pack = jnp.concatenate(
        [
            gain_grad.reshape(-1), xtaps[: CONV + 1].reshape(-1), bctaps[: CONV + 1].reshape(-1),
            ggg.reshape(-1), smalls[:3].reshape(-1),
        ]
    )
    size = -(-pack.shape[0] // (n * LANES)) * LANES
    pack = jnp.pad(pack, (0, n * size - pack.shape[0])).reshape(n, size)
    reduced = jnp.sum(exchange(jnp.concatenate([dt_rows, pack], axis=1).reshape(n, 1, -1)), axis=0)
    grad_dt = jnp.transpose(reduced[0, : heads * rows].reshape(heads, rows))
    spreadout = jnp.broadcast_to(reduced[:, heads * rows :].reshape(1, 1, size), (n, 1, size))
    every = exchange(spreadout).reshape(-1)

    pieces = []
    at = 0
    for count in (width, CONV * inner, inner, CONV * 2 * STATE, 2 * STATE, inner, LANES, LANES, LANES):
        pieces.append(every[at : at + count])
        at += count
    g_norm, g_xw, g_xb, g_bw, g_bb, g_gate, g_step, g_rate, g_skip = pieces
    return (
        hidden_out.reshape(batch, length, width),
        grad_in.reshape(batch, length, width),
        g_norm,
        grad_z,
        grad_x,
        grad_bc,
        grad_dt,
        g_xw.reshape(CONV, inner),
        g_xb,
        g_bw.reshape(CONV, 2 * STATE),
        g_bb,
        g_step[:heads],
        g_rate[:heads],
        g_skip[:heads],
        g_gate,
        grad_out_t.T,
    )


def solution(mesh):
    placed = (
        P(None, "seq", None),
        P(),
        P(None, "head"),
        P(None, "head"),
        P(),
        P(None, "head"),
        P(None, "head"),
        P("head"),
        P(),
        P(),
        P("head"),
        P("head"),
        P("head"),
        P("head"),
        P("head", None),
        P(None, "seq", None),
    )
    return jax.shard_map(
        body,
        mesh=mesh,
        in_specs=placed,
        out_specs=(
            P(None, "seq", None),
            P(None, "seq", None),
            P(),
            P("seq", "head"),
            P("seq", "head"),
            P(("seq", "head"), None),
            P("seq", "head"),
            P(None, "head"),
            P("head"),
            P(),
            P(),
            P("head"),
            P("head"),
            P("head"),
            P("head"),
            P("head", "seq"),
        ),
        check_vma=False,
    )
```

time: 854 us -> 252 us (0.30)
  waiting for transfers between devices: 549 us -> 48.4 us
  blocking collectives: 126 us -> 30.9 us
  Pallas kernels: 0 us -> 63.3 us
  starting transfers between devices: 6.94 us -> 67.7 us
  matrix products: 54.3 us -> 0 us
  other arithmetic: 52.3 us -> 14.3 us
  local copies, waits for them, and re-layouts: 46.1 us -> 24.2 us
  between operations: 15.2 us -> 1.43 us
    reduce_scatter x4 -> x0, waiting for transfers between devices: 292 us -> none  [the longest x1 97.6 us: body(): lax.psum_scatter(matmul_tn(normed_rows, gate_bf), 'seq', scatter_dimensio...]
    all_gather x2 -> x0, waiting for transfers between devices: 175 us -> none  [prefix(): gathered = jax.tree.map(lambda a: lax.all_gather(a, axis), part)]
    psum x3 -> x0, blocking collectives: 84.5 us -> none  [the longest x1 78.3 us: body(): lax.psum((grad_norm_gain, grad_conv_x_weight, grad_conv_x_bias, grad_conv...]
    pallas_call x0 -> x18, Pallas kernels: none -> 63.3 us  [call(): pl.pallas_call(kernel, out_shape=tuple(outs), in_specs=specs, out_specs=t...]
    unnamed x10 -> x0, waiting for transfers between devices: 53.6 us -> none
    dot_general x26 -> x0, matrix products: 53.3 us -> none  [the longest x4 10.2 us: matmul_tn(): lax.dot_general(left, right, (((0,), (0,)), ((), ())), preferred_element_...]
    all_gather x1 -> x0, blocking collectives: 42 us -> none  [prefix(): gathered = jax.tree.map(lambda a: lax.all_gather(a, axis), part)]
    ppermute x2 -> x29, starting transfers between devices: 6.16 us -> 40.8 us  [the longest x22 32.9 us: partner(): return lax.ppermute(value, 'seq', [(i, i ^ bit) for i in range(peers)])]
  transfers between devices with their start and end apart: 11 -> 35, of which waited for: 10 -> 11; matrix products, arithmetic and copies ran while one was open for 8% -> 12% of each run, Pallas kernels for 0% -> 19%
where the time goes in v1:
time: 252 us; the launch traced here: 250 us
  starting transfers between devices  67.7 us (27%)
  Pallas kernels  63.3 us (25%)
  waiting for transfers between devices  48.4 us (19%)
  blocking collectives  30.9 us (12%)
  local copies, waits for them, and re-layouts  24.2 us (10%)
  other arithmetic  14.3 us (6%)
    pallas_call x18, Pallas kernels, call(): pl.pallas_call(kernel, out_shape=tuple(outs), in_specs=specs, out_specs=t...  63.3 us
    ppermute x22, starting transfers between devices, partner(): return lax.ppermute(value, 'seq', [(i, i ^ bit) for i in range(peers)])  32.9 us
    all_to_all x2, blocking collectives, exchange(): return lax.all_to_all(value, 'seq', 0, 0, tiled=True)  30.9 us
    all_to_all x6, starting transfers between devices, exchange(): return lax.all_to_all(value, 'seq', 0, 0, tiled=True)  26.9 us
    ppermute x22, waiting for transfers between devices, partner(): return lax.ppermute(value, 'seq', [(i, i ^ bit) for i in range(peers)])  25 us
    all_to_all x6, waiting for transfers between devices, exchange(): return lax.all_to_all(value, 'seq', 0, 0, tiled=True)  22 us
    unnamed x63, local copies, waits for them, and re-layouts  9.28 us
    ppermute x3, starting transfers between devices, shifted(): lax.ppermute(value, 'seq', [(i, i + by) for i in range(peers) if 0 <= i +...  7.6 us
  transfers between devices with their start and end apart: 35, of which 11 were waited for; matrix products, arithmetic and copies ran while one was open for 12% of the time, Pallas kernels for 19%

profile of v1, /device:TPU:0, one launch (start us, length us, event | category | flops | bytes accessed | tf_op | source)
XLA Modules:
  0.0 250.4 jit_solution(8095901260676963538)
XLA Ops:
  1.4 4.9 %collective-permute-start = (f32[8,1024]{1,0:T(8,128)S(1)}, f32[8,1024]{1,0:T(8,128)S(1)}, u32[]{:S(2)}, u32[]{:S(2)}) collective-permute-start(f32[8,1024]{1,0:T(8,128)S(1)} %slice_bitcast_fusion), channel_id=1, source_target_pairs={{0,2},{2,4},{4,6},{6,8},{8,10},{10,12},{12,14},{14,16},{16,18},{18... | collective-permute-start | bytes 98312 | tf_op jit(solution)/shard_map/ppermute | solution.py:425
  9.8 6.1 %front.1 = (f32[128,1]{1,0:T(8,128)}, f32[136,1024]{1,0:T(8,128)}, f32[128,1024]{1,0:T(8,128)}, bf16[128,1024]{1,0:T(8,128)(2,1)}, f32[136,256]{1,0:T(8,128)}, /...) custom-call(f32[128,1024]{1,0:T(8,128)} %bitcast.39, ...), custom_call_target="tpu_custom_call" | custom-call | flops 335544320 | bytes 6372480 | tf_op jit(solution)/shard_map/front/pallas_call | solution.py:63
  16.6 13.6 %all_to_all.40 = f32[16,1,128]{2,1,0:T(1,128)} all-to-all(f32[16,1,128]{2,1,0:T(1,128)S(1)} %broadcast_in_dim.20), channel_id=1, replica_groups=mesh['seq'=16,'head'=2] {'seq'}, dimensions={0} | all-to-all | bytes 16384 | tf_op jit(solution)/shard_map/all_to_all | solution.py:433
  30.2 17.3 %all_to_all.41.refs_0_ = f32[16,8,1024]{2,1,0:T(8,128)} all-to-all(f32[16,8,1024]{2,1,0:T(8,128)} %bitcast.49), channel_id=1, replica_groups=mesh['seq'=16,'head'=2] {'seq'}, dimensions={0} | all-to-all | bytes 1048576 | tf_op jit(solution)/shard_map/all_to_all | solution.py:433
  49.8 3.9 %all-to-all-start.2 = ((f32[16,8,1024]{2,1,0:T(8,128)}), f32[16,8,1024]{2,1,0:T(8,128)S(1)}, u32[]{:S(2)}, u32[]{:S(2)}) async-start(f32[16,8,1024]{2,1,0:T(8,128)} %scan.2), calls=%async_computation.2 | async-start | bytes 1048576 | tf_op jit(solution)/shard_map/all_to_all | solution.py:433
  54.9 3.4 %left.1 = (bf16[128,1024]{1,0:T(8,128)(2,1)}, bf16[1024,128]{1,0:T(8,128)(2,1)}, f32[512,128]{1,0:T(8,128)}, f32[512,128]{1,0:T(8,128)}, bf16[1024,128]{1,0:T(8,...) custom-call(s32[16]{0:T(128)} %broadcast_xor_fusion.refs_0_, f32[128,1024]{1,0:T(8,128)} %bitcast.40, ...), custom_call_target="tpu_custom_call" | custom-call | bytes 2887744 | tf_op jit(solution)/shard_map/left/pallas_call | solution.py:63
  58.4 5.4 %local.1 = (f32[128,1024]{1,0:T(8,128)}, f32[128,1024]{1,0:T(8,128)}, f32[128,1024]{1,0:T(8,128)}, bf16[16,128,128]{2,1,0:T(8,128)(2,1)}, bf16[16,128,128]{2,1,0:T(8,128)(2,1)}) custom-call(bf16[128,1024]{1,0:T(8,128)(2,1)} %get-tuple-element.88.refs_0_.refs_5_, bf16[1024,1024]{1,0:T(8,128)(2,1)} %refs_1_.5, f32[128,1024]{1,0:T(8,128)} %bitcast.46, ...), custom_call_target="tpu_custom_call" | custom-call | flops 805306368 | bytes 7954432 | tf_op jit(solution)/shard_map/local/pallas_call | solution.py:63
  63.8 3.5 %all-to-all-done.2 = f32[16,8,1024]{2,1,0:T(8,128)S(1)} async-done(((f32[16,8,1024]{2,1,0:T(8,128)}), f32[16,8,1024]{2,1,0:T(8,128)S(1)}, u32[]{:S(2)}, u32[]{:S(2)}) %all-to-all-start.2) | async-done | bytes 524320 | tf_op jit(solution)/shard_map/all_to_all | solution.py:433
  68.1 3.5 %gate.1 = (f32[128,1024]{1,0:T(8,128)}, f32[128,1024]{1,0:T(8,128)}, f32[128,1024]{1,0:T(8,128)}, f32[128,128]{1,0:T(8,128)}) custom-call(f32[128,1024]{1,0:T(8,128)} %bitcast.42, f32[128,1024]{1,0:T(8,128)} %get-tuple-element.94.refs_1_, bf16[128,1024]{1,0:T(8,128)(2,1)} %get-tuple-element.90.refs_5_.refs_2_.refs_7_.refs_3_, ...), custom_call_target="tpu_custom_call" | custom-call | bytes 4177920 | tf_op jit(solution)/shard_map/gate/pallas_call | solution.py:63
  73.8 4.5 %turn.1 = (f32[128,1024]{1,0:T(8,128)}, f32[128,1024]{1,0:T(8,128)}, bf16[128,1024]{1,0:T(8,128)(2,1)}, bf16[128,1024]{1,0:T(8,128)(2,1)}, f32[128,512]{1,0:T(8,...) custom-call(f32[128,128]{1,0:T(8,128)} %get-tuple-element.97.refs_0_, ...), custom_call_target="tpu_custom_call" | custom-call | bytes 5980160 | tf_op jit(solution)/shard_map/turn/pallas_call | solution.py:63
  78.3 3.9 %all-to-all-start.3 = ((f32[16,8,1024]{2,1,0:T(8,128)}), f32[16,8,1024]{2,1,0:T(8,128)S(1)}, u32[]{:S(2)}, u32[]{:S(2)}) async-start(f32[16,8,1024]{2,1,0:T(8,128)} %bitcast.48), calls=%async_computation.3 | async-start | bytes 1048576 | tf_op jit(solution)/shard_map/all_to_all | solution.py:433
  88.2 8.5 %collective-permute-done.21.refs_1_ = f32[512,128]{1,0:T(8,128)S(1)} collective-permute-done((f32[512,128]{1,0:T(8,128)S(1)}, f32[512,128]{1,0:T(8,128)S(1)}, u32[]{:S(2)}, u32[]{:S(2)}) %collective-permute-start.21) | collective-permute-done | bytes 262176 | tf_op jit(solution)/shard_map/ppermute | solution.py:420
  99.5 3.3 %collective-permute-done.23.refs_4_ = f32[128,512]{1,0:T(8,128)} collective-permute-done((f32[128,512]{1,0:T(8,128)}, f32[128,512]{1,0:T(8,128)}, u32[]{:S(2)}, u32[]{:S(2)}) %collective-permute-start.23) | collective-permute-done | bytes 262176 | tf_op jit(solution)/shard_map/ppermute | solution.py:420
  103.0 3.2 %product.5 = (f32[256,1024]{1,0:T(8,128)}, f32[256,512]{1,0:T(8,128)}, f32[256,512]{1,0:T(8,128)}) custom-call(bf16[1024,128]{1,0:T(8,128)(2,1)} %get-tuple-element.148.refs_0_, f32[512,128]{1,0:T(8,128)} %copy-done.26, f32[512,128]{1,0:T(8,128)} %copy-done.27, bf16[128,1024]{1,0:T(8,128)(2,1)} %get-tuple-element.101.refs_0_.refs_3_, ...), custom_call_target="tpu_custom_call" | custom-call | flops 536870912 | bytes 3670016 | tf_op jit(solution)/shard_map/product/pallas_call | solution.py:63
  112.6 5.2 %all-to-all-start.4 = ((f32[16,8,1024]{2,1,0:T(8,128)}), f32[16,8,1024]{2,1,0:T(8,128)}, u32[]{:S(2)}, u32[]{:S(2)}) async-start(f32[16,8,1024]{2,1,0:T(8,128)} %scan.3), calls=%async_computation.4 | async-start | bytes 1048576 | tf_op jit(solution)/shard_map/all_to_all | solution.py:433
  118.5 3.1 %product.3 = (f32[256,1024]{1,0:T(8,128)}, f32[256,512]{1,0:T(8,128)}, f32[256,512]{1,0:T(8,128)}) custom-call(bf16[1024,128]{1,0:T(8,128)(2,1)} %get-tuple-element.134.refs_0_, f32[512,128]{1,0:T(8,128)} %copy-done.21, f32[512,128]{1,0:T(8,128)} %copy-done.22, bf16[128,1024]{1,0:T(8,128)(2,1)} %get-tuple-element.102.refs_0_.refs_3_, ...), custom_call_target="tpu_custom_call" | custom-call | flops 536870912 | bytes 3670016 | tf_op jit(solution)/shard_map/product/pallas_call | solution.py:63
  125.1 3.0 %out.1 = f32[128,1024]{1,0:T(8,128)} custom-call(bf16[128,1024]{1,0:T(8,128)(2,1)} %get-tuple-element.101.refs_0_.refs_3_, bf16[1024,1024]{1,0:T(8,128)(2,1)} %refs_1_.4), custom_call_target="tpu_custom_call" | custom-call | flops 268435456 | bytes 2883584 | tf_op jit(solution)/shard_map/out/pallas_call | solution.py:63
  128.1 4.0 %back.1 = (f32[128,1024]{1,0:T(8,128)}, f32[128,256]{1,0:T(8,128)}, f32[128,16]{1,0:T(8,128)}, f32[128,16]{1,0:T(8,128)}) custom-call(bf16[16,128,128]{2,1,0:T(8,128)(2,1)} %get-tuple-element.106.refs_0_, bf16[16,128,128]{2,1,0:T(8,128)(2,1)} %get-tuple-element.107.refs_1_, f32[128,1024]{1,0:T(8,128)} %get-tuple-element.108.refs_2_.refs_7_, ...), custom_call_target="tpu_custom_call" | custom-call | flops 100663296 | bytes 3915776 | tf_op jit(solution)/shard_map/back/pallas_call | solution.py:63
  135.9 5.6 %collective-permute-done.11 = f32[256,512]{1,0:T(8,128)} collective-permute-done((f32[256,512]{1,0:T(8,128)}, f32[256,512]{1,0:T(8,128)}, u32[]{:S(2)}, u32[]{:S(2)}) %collective-permute-start.11) | collective-permute-done | bytes 524320 | tf_op jit(solution)/shard_map/ppermute | solution.py:420
  145.3 4.0 %end.1 = (f32[128,1024]{1,0:T(8,128)}, f32[128,256]{1,0:T(8,128)}, f32[128,16]{1,0:T(8,128)}, f32[8,128]{1,0:T(8,128)}) custom-call(f32[128,1024]{1,0:T(8,128)} %bitcast.15.refs_0_, f32[128,1024]{1,0:T(8,128)} %bitcast.44, bf16[128,256]{1,0:T(8,128)(2,1)} %get-tuple-element.89.refs_4_.refs_3_.refs_10_.refs_2_, f32[128,1024]{1,0:T(8,128)} %get-tuple-element.104.refs_3_, ...), custom_call_target="tpu_custom_call" | custom-call | bytes 4608576 | tf_op jit(solution)/shard_map/end/pallas_call | solution.py:63
  161.0 5.1 %collective-permute-start.28 = (f32[64,1024]{1,0:T(8,128)}, f32[64,1024]{1,0:T(8,128)}, u32[]{:S(2)}, u32[]{:S(2)}) collective-permute-start(f32[64,1024]{1,0:T(8,128)} %slice.157), channel_id=1, source_target_pairs={{0,16},{2,18},{4,20},{6,22},{8,24},{10,26},{12,28},{14,30},{16,0},... | collective-permute-start | bytes 786440 | tf_op jit(solution)/shard_map/ppermute | solution.py:420
  166.7 3.1 %xback.1 = (bf16[128,1024]{1,0:T(8,128)(2,1)}, f32[128,512]{1,0:T(8,128)}, f32[128,512]{1,0:T(8,128)}, f32[8,1024]{1,0:T(8,128)}) custom-call(f32[128,1024]{1,0:T(8,128)} %get-tuple-element.118.refs_0_, f32[8,1024]{1,0:T(8,128)} %copy-done.14, f32[136,1024]{1,0:T(8,128)} %get-tuple-element.119.refs_2_, f32[4,1024]{1,0:T(4,128)} %refs_3_.7), custom_call_target="tpu_custom_call" | custom-call | bytes 1949696 | tf_op jit(solution)/shard_map/xback/pallas_call | solution.py:63
  176.0 5.2 %in.1.refs_0_ = f32[128,1024]{1,0:T(8,128)} custom-call(bf16[128,1024]{1,0:T(8,128)(2,1)} %get-tuple-element.102.refs_0_.refs_3_, bf16[1024,1024]{1,0:T(8,128)(2,1)} %refs_1_.5, bf16[128,1024]{1,0:T(8,128)(2,1)} %get-tuple-element.120.refs_2_.refs_3_, bf16[1024,1024]{1,0:T(8,128)(2,1)} %refs_3_.9, f32[128,16]{1,0:T(8,128)} %get-tuple-element.121.refs_4_, ...), custom_call_target="tpu_custom_call" | custom-call | flops 536870912 | bytes 5873668 | tf_op jit(solution)/shard_map/in/pallas_call | solution.py:63
  185.9 3.1 %product.4 = (f32[256,1024]{1,0:T(8,128)}, f32[256,512]{1,0:T(8,128)}, f32[256,512]{1,0:T(8,128)}) custom-call(bf16[1024,128]{1,0:T(8,128)(2,1)} %get-tuple-element.134.refs_0_, f32[512,128]{1,0:T(8,128)} %copy-done.21, f32[512,128]{1,0:T(8,128)} %copy-done.22, bf16[128,1024]{1,0:T(8,128)(2,1)} %get-tuple-element.120.refs_2_.refs_3_, ...), custom_call_target="tpu_custom_call" | custom-call | flops 536870912 | bytes 3670016 | tf_op jit(solution)/shard_map/product/pallas_call | solution.py:63
  194.5 5.5 %all-to-all-start.5 = ((f32[16,1,1664]{2,1,0:T(1,128)}), f32[16,1,1664]{2,1,0:T(1,128)S(1)}, u32[]{:S(2)}, u32[]{:S(2)}) async-start(f32[16,1,1664]{2,1,0:T(1,128)} %copy.41), calls=%async_computation.5 | async-start | bytes 212992 | tf_op jit(solution)/shard_map/all_to_all | solution.py:433
  200.0 3.6 %collective-permute-done.17 = f32[256,512]{1,0:T(8,128)} collective-permute-done((f32[256,512]{1,0:T(8,128)}, f32[256,512]{1,0:T(8,128)}, u32[]{:S(2)}, u32[]{:S(2)}) %collective-permute-start.17) | collective-permute-done | bytes 524320 | tf_op jit(solution)/shard_map/ppermute | solution.py:420
  209.1 4.9 %all-to-all-start.6 = ((f32[16,1,640]{2,1,0:T(1,128)}), f32[16,1,640]{2,1,0:T(1,128)S(1)}, u32[]{:S(2)}, u32[]{:S(2)}) async-start(f32[16,1,640]{2,1,0:T(1,128)} %broadcast_in_dim.23), calls=%async_computation.6 | async-start | bytes 81920 | tf_op jit(solution)/shard_map/all_to_all | solution.py:433
  215.9 6.9 %all-to-all-done.6 = f32[16,1,640]{2,1,0:T(1,128)S(1)} async-done(((f32[16,1,640]{2,1,0:T(1,128)}), f32[16,1,640]{2,1,0:T(1,128)S(1)}, u32[]{:S(2)}, u32[]{:S(2)}) %all-to-all-start.6) | async-done | bytes 40992 | tf_op jit(solution)/shard_map/all_to_all | solution.py:433
  222.8 3.6 %all-to-all-start.7 = ((f32[16,32,256]{2,1,0:T(8,128)}), f32[16,32,256]{2,1,0:T(8,128)S(1)}, u32[]{:S(2)}, u32[]{:S(2)}) async-start(f32[16,32,256]{2,1,0:T(8,128)} %dynamic-slice_bitcast_fusion), calls=%async_computation.7 | async-start | bytes 1048576 | tf_op jit(solution)/shard_map/all_to_all | solution.py:433
  228.0 2.9 %collective-permute-start.20 = (f32[64,1024]{1,0:T(8,128)S(1)}, f32[64,1024]{1,0:T(8,128)S(1)}, u32[]{:S(2)}, u32[]{:S(2)}) collective-permute-start(f32[64,1024]{1,0:T(8,128)S(1)} %slice.144), channel_id=1, source_target_pairs={{0,16},{2,18},{4,20},{6,22},{8,24},{10,26},{12,28},{14,30},{16,0},... | collective-permute-start | bytes 786440 | tf_op jit(solution)/shard_map/ppermute | solution.py:420
  233.9 11.5 %all-to-all-done.7 = f32[16,32,256]{2,1,0:T(8,128)S(1)} async-done(((f32[16,32,256]{2,1,0:T(8,128)}), f32[16,32,256]{2,1,0:T(8,128)S(1)}, u32[]{:S(2)}, u32[]{:S(2)}) %all-to-all-start.7) | async-done | bytes 524320 | tf_op jit(solution)/shard_map/all_to_all | solution.py:433
  246.1 3.5 %collective-permute-done.20 = f32[64,1024]{1,0:T(8,128)S(1)} collective-permute-done((f32[64,1024]{1,0:T(8,128)S(1)}, f32[64,1024]{1,0:T(8,128)S(1)}, u32[]{:S(2)}, u32[]{:S(2)}) %collective-permute-start.20) | collective-permute-done | bytes 262176 | tf_op jit(solution)/shard_map/ppermute | solution.py:420
  (174 shorter events, 80.0 us)
Async XLA Ops:
  49.8 17.6 %all-to-all-start.2 = ((f32[16,8,1024]{2,1,0:T(8,128)}), f32[16,8,1024]{2,1,0:T(8,128)S(1)}, u32[]{:S(2)}, u32[]{:S(2)}) async-start(f32[16,8,1024]{2,1,0:T(8,128)} %scan.2), calls=%async_computation.2 | async-start | bytes 1048576 | tf_op jit(solution)/shard_map/all_to_all | solution.py:433
  78.3 31.3 %all-to-all-start.3 = ((f32[16,8,1024]{2,1,0:T(8,128)}), f32[16,8,1024]{2,1,0:T(8,128)S(1)}, u32[]{:S(2)}, u32[]{:S(2)}) async-start(f32[16,8,1024]{2,1,0:T(8,128)} %bitcast.48), calls=%async_computation.3 | async-start | bytes 1048576 | tf_op jit(solution)/shard_map/all_to_all | solution.py:433
  82.2 14.6 %collective-permute-start.21 = (f32[512,128]{1,0:T(8,128)S(1)}, f32[512,128]{1,0:T(8,128)S(1)}, u32[]{:S(2)}, u32[]{:S(2)}) collective-permute-start(f32[512,128]{1,0:T(8,128)S(1)} %copy-done.25), channel_id=1, source_target_pairs={{0,2},{2,0},{4,6},{6,4},{8,10},{10,8},{12,14},{14,12},{16,18},{18,... | collective-permute-start | bytes 786440 | tf_op jit(solution)/shard_map/ppermute | solution.py:420
  84.1 14.1 %collective-permute-start.22 = (f32[512,128]{1,0:T(8,128)S(1)}, f32[512,128]{1,0:T(8,128)S(1)}, u32[]{:S(2)}, u32[]{:S(2)}) collective-permute-start(f32[512,128]{1,0:T(8,128)S(1)} %copy-done.24), channel_id=1, source_target_pairs={{0,4},{2,6},{4,0},{6,2},{8,12},{10,14},{12,8},{14,10},{16,20},{18,... | collective-permute-start | bytes 786440 | tf_op jit(solution)/shard_map/ppermute | solution.py:420
  85.6 17.2 %collective-permute-start.23 = (f32[128,512]{1,0:T(8,128)}, f32[128,512]{1,0:T(8,128)}, u32[]{:S(2)}, u32[]{:S(2)}) collective-permute-start(f32[128,512]{1,0:T(8,128)} %get-tuple-element.151), channel_id=1, source_target_pairs={{0,2},{2,0},{4,6},{6,4},{8,10},{10,8},{12,14},{14,12},{16,18},{18,... | collective-permute-start | bytes 786440 | tf_op jit(solution)/shard_map/ppermute | solution.py:420
  86.2 16.8 %collective-permute-start.24 = (f32[128,512]{1,0:T(8,128)}, f32[128,512]{1,0:T(8,128)}, u32[]{:S(2)}, u32[]{:S(2)}) collective-permute-start(f32[128,512]{1,0:T(8,128)} %get-tuple-element.152), channel_id=1, source_target_pairs={{0,4},{2,6},{4,0},{6,2},{8,12},{10,14},{12,8},{14,10},{16,20},{18,... | collective-permute-start | bytes 786440 | tf_op jit(solution)/shard_map/ppermute | solution.py:420
  86.3 22.0 %collective-permute-start.7 = (f32[512,128]{1,0:T(8,128)}, f32[512,128]{1,0:T(8,128)S(1)}, u32[]{:S(2)}, u32[]{:S(2)}) collective-permute-start(f32[512,128]{1,0:T(8,128)} %get-tuple-element.135), channel_id=1, source_target_pairs={{0,2},{2,0},{4,6},{6,4},{8,10},{10,8},{12,14},{14,12},{16,18},{18,... | collective-permute-start | bytes 786440 | tf_op jit(solution)/shard_map/ppermute | solution.py:420
  96.7 21.1 %collective-permute-start.8 = (f32[512,128]{1,0:T(8,128)S(1)}, f32[512,128]{1,0:T(8,128)S(1)}, u32[]{:S(2)}, u32[]{:S(2)}) collective-permute-start(f32[512,128]{1,0:T(8,128)S(1)} %copy-done.23), channel_id=1, source_target_pairs={{0,4},{2,6},{4,0},{6,2},{8,12},{10,14},{12,8},{14,10},{16,20},{18,... | collective-permute-start | bytes 786440 | tf_op jit(solution)/shard_map/ppermute | solution.py:420
  98.9 18.9 %collective-permute-start.10 = (f32[128,512]{1,0:T(8,128)}, f32[128,512]{1,0:T(8,128)}, u32[]{:S(2)}, u32[]{:S(2)}) collective-permute-start(f32[128,512]{1,0:T(8,128)} %get-tuple-element.138), channel_id=1, source_target_pairs={{0,4},{2,6},{4,0},{6,2},{8,12},{10,14},{12,8},{14,10},{16,20},{18,... | collective-permute-start | bytes 786440 | tf_op jit(solution)/shard_map/ppermute | solution.py:420
  102.8 15.1 %collective-permute-start.9 = (f32[128,512]{1,0:T(8,128)}, f32[128,512]{1,0:T(8,128)}, u32[]{:S(2)}, u32[]{:S(2)}) collective-permute-start(f32[128,512]{1,0:T(8,128)} %get-tuple-element.137), channel_id=1, source_target_pairs={{0,2},{2,0},{4,6},{6,4},{8,10},{10,8},{12,14},{14,12},{16,18},{18,... | collective-permute-start | bytes 786440 | tf_op jit(solution)/shard_map/ppermute | solution.py:420
  106.2 26.0 %collective-permute-start.25 = (f32[256,512]{1,0:T(8,128)}, f32[256,512]{1,0:T(8,128)S(1)}, u32[]{:S(2)}, u32[]{:S(2)}) collective-permute-start(f32[256,512]{1,0:T(8,128)} %get-tuple-element.154), channel_id=1, source_target_pairs={{0,4},{2,6},{4,0},{6,2},{8,12},{10,14},{12,8},{14,10},{16,20},{18,... | collective-permute-start | bytes 1572872 | tf_op jit(solution)/shard_map/ppermute | solution.py:420
  108.3 23.9 %collective-permute-start.26 = (f32[256,512]{1,0:T(8,128)}, f32[256,512]{1,0:T(8,128)}, u32[]{:S(2)}, u32[]{:S(2)}) collective-permute-start(f32[256,512]{1,0:T(8,128)} %get-tuple-element.155), channel_id=1, source_target_pairs={{0,2},{2,0},{4,6},{6,4},{8,10},{10,8},{12,14},{14,12},{16,18},{18,... | collective-permute-start | bytes 1572872 | tf_op jit(solution)/shard_map/ppermute | solution.py:420
  112.6 32.6 %all-to-all-start.4 = ((f32[16,8,1024]{2,1,0:T(8,128)}), f32[16,8,1024]{2,1,0:T(8,128)}, u32[]{:S(2)}, u32[]{:S(2)}) async-start(f32[16,8,1024]{2,1,0:T(8,128)} %scan.3), calls=%async_computation.4 | async-start | bytes 1048576 | tf_op jit(solution)/shard_map/all_to_all | solution.py:433
  121.7 19.9 %collective-permute-start.11 = (f32[256,512]{1,0:T(8,128)}, f32[256,512]{1,0:T(8,128)}, u32[]{:S(2)}, u32[]{:S(2)}) collective-permute-start(f32[256,512]{1,0:T(8,128)} %get-tuple-element.140), channel_id=1, source_target_pairs={{0,4},{2,6},{4,0},{6,2},{8,12},{10,14},{12,8},{14,10},{16,20},{18,... | collective-permute-start | bytes 1572872 | tf_op jit(solution)/shard_map/ppermute | solution.py:420
  123.6 18.0 %collective-permute-start.12 = (f32[256,512]{1,0:T(8,128)}, f32[256,512]{1,0:T(8,128)}, u32[]{:S(2)}, u32[]{:S(2)}) collective-permute-start(f32[256,512]{1,0:T(8,128)} %get-tuple-element.141), channel_id=1, source_target_pairs={{0,2},{2,0},{4,6},{6,4},{8,10},{10,8},{12,14},{14,12},{16,18},{18,... | collective-permute-start | bytes 1572872 | tf_op jit(solution)/shard_map/ppermute | solution.py:420
  128.1 21.3 %collective-permute-start.2 = (f32[128,1024]{1,0:T(8,128)}, f32[128,1024]{1,0:T(8,128)}, u32[]{:S(2)}, u32[]{:S(2)}) collective-permute-start(f32[128,1024]{1,0:T(8,128)} %out.1), channel_id=1, source_target_pairs={{0,1},{1,0},{2,3},{3,2},{4,5},{5,4},{6,7},{7,6},{8,9},{9,8},{10,11... | collective-permute-start | bytes 1572872 | tf_op jit(solution)/shard_map/ppermute | solution.py:429
  134.5 23.7 %collective-permute-start.27 = (f32[128,1024]{1,0:T(8,128)}, f32[128,1024]{1,0:T(8,128)}, u32[]{:S(2)}, u32[]{:S(2)}) collective-permute-start(f32[128,1024]{1,0:T(8,128)} %slice.155), channel_id=1, source_target_pairs={{0,8},{2,10},{4,12},{6,14},{8,0},{10,2},{12,4},{14,6},{16,24},{18,... | collective-permute-start | bytes 1572872 | tf_op jit(solution)/shard_map/ppermute | solution.py:420
  143.8 37.6 %collective-permute-start.13 = (f32[128,1024]{1,0:T(8,128)}, f32[128,1024]{1,0:T(8,128)}, u32[]{:S(2)}, u32[]{:S(2)}) collective-permute-start(f32[128,1024]{1,0:T(8,128)} %slice.138), channel_id=1, source_target_pairs={{0,8},{2,10},{4,12},{6,14},{8,0},{10,2},{12,4},{14,6},{16,24},{18,... | collective-permute-start | bytes 1572872 | tf_op jit(solution)/shard_map/ppermute | solution.py:420
  152.3 13.8 %collective-permute-start.3 = (f32[8,1024]{1,0:T(8,128)S(1)}, f32[8,1024]{1,0:T(8,128)S(1)}, u32[]{:S(2)}, u32[]{:S(2)}) collective-permute-start(f32[8,1024]{1,0:T(8,128)S(1)} %slice.104), channel_id=1, source_target_pairs={{2,0},{4,2},{6,4},{8,6},{10,8},{12,10},{14,12},{16,14},{18,16},{20... | collective-permute-start | bytes 98312 | tf_op jit(solution)/shard_map/ppermute | solution.py:425
  156.9 15.9 %collective-permute-start.5 = (f32[8,256]{1,0:T(8,128)S(1)}, f32[8,256]{1,0:T(8,128)S(1)}, u32[]{:S(2)}, u32[]{:S(2)}) collective-permute-start(f32[8,256]{1,0:T(8,128)S(1)} %slice.134), channel_id=1, source_target_pairs={{2,0},{4,2},{6,4},{8,6},{10,8},{12,10},{14,12},{16,14},{18,16},{20... | collective-permute-start | bytes 24584 | tf_op jit(solution)/shard_map/ppermute | solution.py:425
  161.0 22.9 %collective-permute-start.28 = (f32[64,1024]{1,0:T(8,128)}, f32[64,1024]{1,0:T(8,128)}, u32[]{:S(2)}, u32[]{:S(2)}) collective-permute-start(f32[64,1024]{1,0:T(8,128)} %slice.157), channel_id=1, source_target_pairs={{0,16},{2,18},{4,20},{6,22},{8,24},{10,26},{12,28},{14,30},{16,0},... | collective-permute-start | bytes 786440 | tf_op jit(solution)/shard_map/ppermute | solution.py:420
  169.8 16.1 %collective-permute-start.15 = (f32[128,512]{1,0:T(8,128)}, f32[128,512]{1,0:T(8,128)}, u32[]{:S(2)}, u32[]{:S(2)}) collective-permute-start(f32[128,512]{1,0:T(8,128)} %get-tuple-element.142), channel_id=1, source_target_pairs={{0,2},{2,0},{4,6},{6,4},{8,10},{10,8},{12,14},{14,12},{16,18},{18,... | collective-permute-start | bytes 786440 | tf_op jit(solution)/shard_map/ppermute | solution.py:420
  170.7 15.1 %collective-permute-start.16 = (f32[128,512]{1,0:T(8,128)}, f32[128,512]{1,0:T(8,128)}, u32[]{:S(2)}, u32[]{:S(2)}) collective-permute-start(f32[128,512]{1,0:T(8,128)} %get-tuple-element.143), channel_id=1, source_target_pairs={{0,4},{2,6},{4,0},{6,2},{8,12},{10,14},{12,8},{14,10},{16,20},{18,... | collective-permute-start | bytes 786440 | tf_op jit(solution)/shard_map/ppermute | solution.py:420
  181.3 9.0 %collective-permute-start.6 = (f32[128,1024]{1,0:T(8,128)}, f32[128,1024]{1,0:T(8,128)}, u32[]{:S(2)}, u32[]{:S(2)}) collective-permute-start(f32[128,1024]{1,0:T(8,128)} %in.1.refs_0_), channel_id=1, source_target_pairs={{0,1},{1,0},{2,3},{3,2},{4,5},{5,4},{6,7},{7,6},{8,9},{9,8},{10,11... | collective-permute-start | bytes 1572872 | tf_op jit(solution)/shard_map/ppermute | solution.py:429
  183.3 43.2 %collective-permute-start.14 = (f32[64,1024]{1,0:T(8,128)}, f32[64,1024]{1,0:T(8,128)S(1)}, u32[]{:S(2)}, u32[]{:S(2)}) collective-permute-start(f32[64,1024]{1,0:T(8,128)} %slice.140), channel_id=1, source_target_pairs={{0,16},{2,18},{4,20},{6,22},{8,24},{10,26},{12,28},{14,30},{16,0},... | collective-permute-start | bytes 786440 | tf_op jit(solution)/shard_map/ppermute | solution.py:420
  189.0 14.6 %collective-permute-start.17 = (f32[256,512]{1,0:T(8,128)}, f32[256,512]{1,0:T(8,128)}, u32[]{:S(2)}, u32[]{:S(2)}) collective-permute-start(f32[256,512]{1,0:T(8,128)} %get-tuple-element.145), channel_id=1, source_target_pairs={{0,4},{2,6},{4,0},{6,2},{8,12},{10,14},{12,8},{14,10},{16,20},{18,... | collective-permute-start | bytes 1572872 | tf_op jit(solution)/shard_map/ppermute | solution.py:420
  189.1 14.6 %collective-permute-start.18 = (f32[256,512]{1,0:T(8,128)}, f32[256,512]{1,0:T(8,128)}, u32[]{:S(2)}, u32[]{:S(2)}) collective-permute-start(f32[256,512]{1,0:T(8,128)} %get-tuple-element.146), channel_id=1, source_target_pairs={{0,2},{2,0},{4,6},{6,4},{8,10},{10,8},{12,14},{14,12},{16,18},{18,... | collective-permute-start | bytes 1572872 | tf_op jit(solution)/shard_map/ppermute | solution.py:420
  194.5 13.8 %all-to-all-start.5 = ((f32[16,1,1664]{2,1,0:T(1,128)}), f32[16,1,1664]{2,1,0:T(1,128)S(1)}, u32[]{:S(2)}, u32[]{:S(2)}) async-start(f32[16,1,1664]{2,1,0:T(1,128)} %copy.41), calls=%async_computation.5 | async-start | bytes 212992 | tf_op jit(solution)/shard_map/all_to_all | solution.py:433
  205.9 22.0 %collective-permute-start.19 = (f32[128,1024]{1,0:T(8,128)}, f32[128,1024]{1,0:T(8,128)S(1)}, u32[]{:S(2)}, u32[]{:S(2)}) collective-permute-start(f32[128,1024]{1,0:T(8,128)} %slice.142), channel_id=1, source_target_pairs={{0,8},{2,10},{4,12},{6,14},{8,0},{10,2},{12,4},{14,6},{16,24},{18,... | collective-permute-start | bytes 1572872 | tf_op jit(solution)/shard_map/ppermute | solution.py:420
  209.1 13.7 %all-to-all-start.6 = ((f32[16,1,640]{2,1,0:T(1,128)}), f32[16,1,640]{2,1,0:T(1,128)S(1)}, u32[]{:S(2)}, u32[]{:S(2)}) async-start(f32[16,1,640]{2,1,0:T(1,128)} %broadcast_in_dim.23), calls=%async_computation.6 | async-start | bytes 81920 | tf_op jit(solution)/shard_map/all_to_all | solution.py:433
  222.8 22.6 %all-to-all-start.7 = ((f32[16,32,256]{2,1,0:T(8,128)}), f32[16,32,256]{2,1,0:T(8,128)S(1)}, u32[]{:S(2)}, u32[]{:S(2)}) async-start(f32[16,32,256]{2,1,0:T(8,128)} %dynamic-slice_bitcast_fusion), calls=%async_computation.7 | async-start | bytes 1048576 | tf_op jit(solution)/shard_map/all_to_all | solution.py:433
  228.0 21.7 %collective-permute-start.20 = (f32[64,1024]{1,0:T(8,128)S(1)}, f32[64,1024]{1,0:T(8,128)S(1)}, u32[]{:S(2)}, u32[]{:S(2)}) collective-permute-start(f32[64,1024]{1,0:T(8,128)S(1)} %slice.144), channel_id=1, source_target_pairs={{0,16},{2,18},{4,20},{6,22},{8,24},{10,26},{12,28},{14,30},{16,0},... | collective-permute-start | bytes 786440 | tf_op jit(solution)/shard_map/ppermute | solution.py:420
  (32 other events, 276.6 us)

commit v2 on v1

v2 whole, which is shorter than its diff:
```python
import functools

import jax
import jax.numpy as jnp
from jax import lax
from jax.experimental import pallas as pl
from jax.experimental.pallas import tpu as pltpu
from jax.sharding import PartitionSpec as P

INNER = 2048
HEADDIM = 64
STATE = 128
CONV = 4
EDGE = 8
LANES = 128

EPS = 1e-05
HIGHEST = lax.Precision.HIGHEST
F32 = jnp.float32
BF16 = jnp.bfloat16

NN = (((1,), (0,)), ((), ()))
NT = (((1,), (1,)), ((), ()))
TN = (((0,), (0,)), ((), ()))


def dot(left, right, dims=NN, precision=None):
    return lax.dot_general(left, right, dims, precision=precision, preferred_element_type=F32)


class Held:
    def __init__(self, ref, copy):
        self.ref, self.copy = ref, copy
        self.shape, self.dtype = ref.shape, ref.dtype

    def ready(self):
        if self.copy is not None:
            self.copy.wait()
            self.copy = None
        return self.ref

    def __getitem__(self, index):
        return self.ready()[index]


class Result:
    def __init__(self, ref, copy):
        self.ref, self.copy, self.started = ref, copy, False
        self.shape, self.dtype = ref.shape, ref.dtype

    def __getitem__(self, index):
        return self.ref[index]

    def __setitem__(self, index, value):
        self.ref[index] = value

    def flush(self):
        if not self.started:
            self.copy.start()
            self.started = True


def call(body, outs, *args, scratch=(), name=None, flops=0):
    moved = sum(a.size * a.dtype.itemsize for a in args)
    moved += sum(o.size * o.dtype.itemsize for o in outs)
    ins = len(args)
    buffers = [pltpu.VMEM(a.shape, a.dtype) for a in (*args, *outs)]
    count = len(buffers)

    def kernel(*refs):
        arrays, held, sems, own = refs[:count], refs[count : 2 * count], refs[2 * count], refs[2 * count + 1 :]
        given = [
            Held(held[k], pltpu.make_async_copy(arrays[k], held[k], sems.at[k])) for k in range(ins)
        ]
        for item in given:
            item.copy.start()
        results = [
            Result(held[k], pltpu.make_async_copy(held[k], arrays[k], sems.at[k])) for k in range(ins, count)
        ]
        body(*given, *results, *own)
        for item in given:
            item.ready()
        for item in results:
            item.flush()
        for item in results:
            item.copy.wait()

    anywhere = pl.BlockSpec(memory_space=pl.ANY)
    return pl.pallas_call(
        kernel,
        out_shape=tuple(outs),
        in_specs=[anywhere] * ins,
        out_specs=tuple(anywhere for _ in outs),
        scratch_shapes=buffers + [pltpu.SemaphoreType.DMA((count,))] + list(scratch),
        name=name,
        compiler_params=pltpu.CompilerParams(vmem_limit_bytes=62 * 1024 * 1024),
        cost_estimate=pl.CostEstimate(flops=flops, bytes_accessed=moved, transcendentals=0),
    )(*args)


def f32(*shape):
    return jax.ShapeDtypeStruct(shape, F32)


def bf16(*shape):
    return jax.ShapeDtypeStruct(shape, BF16)


def sigmoid(values):
    return 1.0 / (1.0 + jnp.exp(-values))


def silu_slope(values):
    logistic = sigmoid(values)
    return logistic * (1.0 + values * (1.0 - logistic))


def split3(values):
    high = values.astype(BF16)
    rest = values - high.astype(F32)
    mid = rest.astype(BF16)
    low = (rest - mid.astype(F32)).astype(BF16)
    return high, mid, low


def head_onehot(heads, inner, copies):
    rows = row_ids(copies * heads, inner) % heads
    return (col_ids(copies * heads, inner) // HEADDIM == rows).astype(F32).astype(BF16)


def expand(values, inner):
    return dot(jnp.concatenate(split3(values), axis=1), head_onehot(values.shape[1], inner, 3))


def head_sums(values, onehot):
    high, mid, low = split3(values)
    return dot(high, onehot, NT) + dot(mid, onehot, NT) + dot(low, onehot, NT)


def to_chunks(state, out):
    rows = STATE // out.shape[0]
    for j in range(out.shape[0]):
        for t in range(state.shape[1] // LANES):
            out[j, t * rows : (t + 1) * rows, :] = state[
                j * rows : (j + 1) * rows, t * LANES : (t + 1) * LANES
            ]


def from_chunks(parts, state):
    rows = STATE // parts.shape[0]
    for j in range(parts.shape[0]):
        for t in range(state.shape[1] // LANES):
            state[j * rows : (j + 1) * rows, t * LANES : (t + 1) * LANES] = parts[
                j, t * rows : (t + 1) * rows, :
            ]


def row_ids(rows, cols):
    return lax.broadcasted_iota(jnp.int32, (rows, cols), 0)


def col_ids(rows, cols):
    return lax.broadcasted_iota(jnp.int32, (rows, cols), 1)


def left_kernel(bits, hid, gain, og, normed, inv_o, nfull, nsend_a, nsend_b, gfull, gsend_a, gsend_b, tr, tmp):
    n = 1 << bits
    place = lax.axis_index("seq")
    h = hid[...]
    inv = lax.rsqrt(jnp.mean(h * h, axis=-1, keepdims=True) + EPS)
    inv_o[...] = inv
    nb = (h * inv * gain[...]).astype(BF16)
    normed[...] = nb
    rows = h.shape[1] // n
    quarter = h.shape[1] // 4
    for which, full, send_a, send_b in ((0, nfull, nsend_a, nsend_b), (1, gfull, gsend_a, gsend_b)):
        src = og[...].astype(BF16) if which else nb
        tr[...] = src.astype(F32).T
        for p in range(n):
            c = place ^ sum(((p >> (bits - 1 - b)) & 1) << b for b in range(bits))
            tmp[p * rows : (p + 1) * rows, :] = tr[pl.ds(pl.multiple_of(c * rows, rows), rows), :]
        send_a[...] = tmp[2 * quarter :, :]
        send_a.flush()
        send_b[0:quarter, :] = tmp[quarter : 2 * quarter, :]
        send_b[quarter:, :] = tmp[3 * quarter :, :]
        send_b.flush()
        full[...] = tmp[...].astype(BF16)
        full.flush()


def front_kernel(
    normed, edge, gain, wdt, sbias, lrate, wbc, cbw, cbb, cxw, cxb, wx,
    xpad, xconv, xact, bcpad, bcconv, bcact, upre, dts, cums, cumst, dtst, sloc, xw_o,
    nb_s, st_s,
):
    length = normed.shape[0]
    heads = sbias.shape[1]
    inner = wx.shape[1]
    e = edge[...]
    einv = lax.rsqrt(jnp.mean(e * e, axis=-1, keepdims=True) + EPS)
    nb_s[0:EDGE, :] = (e * einv * gain[...]).astype(BF16).astype(F32)
    nb_s[EDGE:, :] = normed[...].astype(F32)
    nb = nb_s[...].astype(BF16)
    u = dot(normed[...], wdt[...], NT) + sbias[...]
    upre[...] = u
    dt = jnp.maximum(u, 0.0) + jnp.log1p(jnp.exp(-jnp.abs(u)))
    dts[...] = dt
    rate = -jnp.exp(lrate[...])
    lower = (row_ids(length, length) >= col_ids(length, length)).astype(F32)
    cum = dot(lower, dt * rate, precision=HIGHEST)
    eye = (row_ids(heads, heads) == col_ids(heads, heads)).astype(F32)
    cums[...] = cum
    cumst[...] = dot(eye, cum, NT, precision=HIGHEST)
    dtst[...] = dot(eye, dt, NT, precision=HIGHEST)
    for item in (upre, dts, cums, cumst, dtst):
        item.flush()
    tot = cum[length - 1 :, :]
    fac = expand(jnp.exp(tot - cum) * dt, inner)
    leaving = expand(jnp.broadcast_to(jnp.exp(tot), (inner // LANES, heads)), inner)
    bcpad[...] = dot(nb, wbc[...])
    conv = cbb[...] + cbw[0:1, :] * bcpad[EDGE - 3 : EDGE - 3 + length, :]
    for k in range(1, CONV):
        conv = conv + cbw[k : k + 1, :] * bcpad[EDGE - 3 + k : EDGE - 3 + k + length, :]
    bcconv[...] = conv
    bca = (conv * sigmoid(conv)).astype(BF16)
    bcact[...] = bca
    for item in (bcpad, bcconv, bcact):
        item.flush()
    b = bca[:, 0:STATE]
    tile = 256
    for j in range(inner // tile):
        cols = slice(j * tile, (j + 1) * tile)
        xpad[:, cols] = dot(nb, wx[:, cols])
        conv = cxb[:, cols] + cxw[0:1, cols] * xpad[EDGE - 3 : EDGE - 3 + length, cols]
        for k in range(1, CONV):
            conv = conv + cxw[k : k + 1, cols] * xpad[EDGE - 3 + k : EDGE - 3 + k + length, cols]
        xconv[:, cols] = conv
        xb = (conv * sigmoid(conv)).astype(BF16)
        xact[:, cols] = xb
        xw = (fac[:, cols] * xb.astype(F32)).astype(BF16)
        xw_o[:, cols] = xw
        st_s[:, cols] = dot(b, xw, TN)
    for item in (xpad, xconv, xact, xw_o):
        item.flush()
    to_chunks(st_s, sloc)
    tiles = inner // LANES
    row = row_ids(tiles, LANES)
    packed = jnp.zeros((tiles, LANES), F32)
    for t in range(tiles):
        packed = packed + jnp.where(row == t, leaving[:, t * LANES : (t + 1) * LANES], 0.0)
    for j in range(sloc.shape[0]):
        sloc[j, sloc.shape[1] - tiles :, :] = packed


def scan_rows(parts, decs, out, reverse):
    n, rows, _ = out.shape
    tiles = decs(0).shape[0]
    each = rows // tiles

    def one(step, states):
        j = n - 1 - step if reverse else step
        dec = decs(j)
        after = []
        for t, state in enumerate(states):
            out[j, t * each : (t + 1) * each, :] = state
            after.append(dec[t : t + 1, :] * state + parts[j, t * each : (t + 1) * each, :])
        return tuple(after)

    lax.fori_loop(0, n, one, (jnp.zeros((each, LANES), F32),) * tiles)


def scan_kernel(parts, out, dec):
    ref, rows = parts.ready(), out.shape[1]
    dec[...] = ref[:, rows:, :]
    dec.flush()
    scan_rows(ref, lambda j: dec[j], out, False)


def scan_back_kernel(parts, dec, out):
    ref, decs = parts.ready(), dec.ready()
    scan_rows(ref, lambda j: decs[j], out, True)


def local_kernel(cums, cumst, dtst, bcact, xact, normed, wz, gbf, wout, gate_pre, ngrad, yloc, mats, decs):
    length = normed.shape[0]
    bca = bcact[...]
    b, c = bca[:, 0:STATE], bca[:, STATE:]
    cb = dot(c, b, NT)
    mask = row_ids(length, length) >= col_ids(length, length)
    lane = col_ids(length, LANES)
    for j in range(xact.shape[1] // LANES):
        xp = xact[:, j * LANES : (j + 1) * LANES]
        y = None
        for half in range(2):
            head = 2 * j + half
            gap = cums[:, head : head + 1] - cumst[head : head + 1, :]
            dec = jnp.where(mask, jnp.exp(jnp.where(mask, gap, 0.0)), 0.0) * dtst[head : head + 1, :]
            m = (cb * dec).astype(BF16)
            decs[head] = dec.astype(BF16)
            mats[head] = m
            xh = jnp.where((lane < HEADDIM) == (half == 0), xp, jnp.zeros_like(xp))
            part = dot(m, xh)
            y = part if y is None else y + part
        yloc[:, j * LANES : (j + 1) * LANES] = y
    for item in (decs, mats, yloc):
        item.flush()
    gate_pre[...] = dot(normed[...], wz[...])
    gate_pre.flush()
    ngrad[...] = dot(gbf[...].astype(BF16), wout[...], NT)


def gate_kernel(cums, skip, ggain, parts, bcact, xact, yloc, gate_pre, ngrad, sums, yns, sin, st_s):
    inner = xact.shape[1]
    from_chunks(parts.ready(), st_s)
    state = st_s[...].astype(BF16)
    sin[...] = state
    sin.flush()
    c = bcact[...][:, STATE:]
    y0 = yloc[...] + expand(jnp.exp(cums[...]), inner) * dot(c, state)
    yns[...] = y0
    yns.flush()
    gp = gate_pre[...]
    g = (y0 + expand(skip[...], inner) * xact[...].astype(F32)) * (gp * sigmoid(gp))
    s1 = jnp.sum(g * g, axis=-1, keepdims=True)
    s2 = jnp.sum(ngrad[...] * ggain[...] * g, axis=-1, keepdims=True)
    lane = col_ids(g.shape[0], LANES)
    sums[...] = jnp.where(lane == 0, s1, jnp.where(lane == 1, s2, 0.0))


def gate_values(sums, other, skip, ggain, yns, xact, gate_pre, ngrad):
    both = sums[...] + other[...]
    rms = lax.rsqrt(both[:, 0:1] / INNER + EPS)
    hat_dot = rms * both[:, 1:2]
    x = xact[...].astype(F32)
    y = yns[...] + expand(skip[...], x.shape[1]) * x
    gp = gate_pre[...]
    sg = sigmoid(gp)
    hat = y * (gp * sg) * rms
    ng = ngrad[...]
    d = rms * (ng * ggain[...] - hat * hat_dot / INNER)
    return x, y, gp, sg, hat, ng, d


def turn_kernel(sums, other, cums, skip, ggain, bcact, xact, yns, gate_pre, ngrad, dsin, dyc, ygrad, st_s):
    x, y, gp, sg, hat, ng, d = gate_values(sums, other, skip, ggain, yns, xact, gate_pre, ngrad)
    yg = d * (gp * sg)
    ygrad[...] = yg
    ygrad.flush()
    dy = (yg * expand(jnp.exp(cums[...]), x.shape[1])).astype(BF16)
    dyc[...] = dy
    dyc.flush()
    st_s[...] = dot(bcact[...][:, STATE:], dy, TN)
    to_chunks(st_s, dsin)


def turn_rest_kernel(
    sums, other, skip, ggain, xact, yns, gate_pre, ngrad, ygrad, gn, gn_a, gn_b, gg, gg_a, gg_b, ggg, skp,
):
    x, y, gp, sg, hat, ng, d = gate_values(sums, other, skip, ggain, yns, xact, gate_pre, ngrad)
    gate_normed = (hat * ggain[...]).astype(BF16)
    gn[...] = gate_normed
    mid = gate_normed.shape[1] // 2
    gn_a[...] = gate_normed[:, :mid].astype(F32)
    gn_b[...] = gate_normed[:, mid:].astype(F32)
    for item in (gn, gn_a, gn_b):
        item.flush()
    gate_grad = (d * y * (sg * (1.0 + gp * (1.0 - sg)))).astype(BF16)
    gg[...] = gate_grad
    gg_a[...] = gate_grad[:, :mid].astype(F32)
    gg_b[...] = gate_grad[:, mid:].astype(F32)
    for item in (gg, gg_a, gg_b):
        item.flush()
    ggg[...] = jnp.sum(ng * hat, axis=0, keepdims=True)
    skp[...] = jnp.sum(ygrad[...] * x, axis=0, keepdims=True)


def back_kernel(xact, ygrad, mats, decs, bcact, dyc, sin, yns, bc_part, diff, kloc_o, dxloc):
    length = xact.shape[0]
    for item in (xact, ygrad, mats, decs, bcact, dyc, sin, yns):
        item.ready()
    lane = col_ids(length, LANES)
    dcb = jnp.zeros((length, length), F32)
    for j in range(xact.shape[1] // LANES):
        cols = slice(j * LANES, (j + 1) * LANES)
        xp = xact[:, cols]
        dyp = ygrad[:, cols].astype(BF16)
        dx = None
        for half in range(2):
            head = 2 * j + half
            dyh = jnp.where((lane < HEADDIM) == (half == 0), dyp, jnp.zeros_like(dyp))
            dcb = dcb + dot(dyh, xp, NT) * decs[head].astype(F32)
            part = dot(mats[head], dyh, TN)
            dx = part if dx is None else dx + part
        dxloc[:, cols] = dx
    dxloc.flush()
    bca = bcact[...]
    b, c = bca[:, 0:STATE], bca[:, STATE:]
    dcbb = dcb.astype(BF16)
    bc_part[:, 0:STATE] = dot(dcbb, c, TN)
    bc_part[:, STATE:] = dot(dcbb, b) + dot(dyc[...], sin[...], NT)
    bc_part.flush()
    onehot = head_onehot(mats.shape[0], xact.shape[1], 1)
    rows = head_sums(ygrad[...].astype(BF16).astype(F32) * yns[...], onehot)
    kloc = head_sums(xact[...].astype(F32) * dxloc[...], onehot)
    diff[...] = rows - kloc
    kloc_o[...] = kloc


def end_kernel(
    parts, bcact, cums, dts, skip, xw, xact, dxloc, ygrad, xconv, bc_part, bcconv, sin, diff, kloc_i, upre, lrate, skp,
    xcg, bcg, edge, dstep, smalls, st_s,
):
    length, inner = xact.shape
    heads = upre.shape[1]
    from_chunks(parts.ready(), st_s)
    dsb = st_s[...].astype(BF16)
    cum = cums[...]
    dt = dts[...]
    tot = cum[length - 1 :, :]
    dxst = expand(jnp.exp(tot - cum) * dt, inner) * dot(bcact[...][:, 0:STATE], dsb)
    x = xact[...].astype(F32)
    grad = dxloc[...] + dxst + expand(skip[...], inner) * ygrad[...]
    grad = grad * silu_slope(xconv[...])
    xcg[...] = grad
    xcg.flush()
    edge[:, 0:inner] = grad[0:EDGE, :]
    slope = silu_slope(bcconv[...])
    bcg[:, 0:STATE] = (bc_part[:, 0:STATE] + dot(xw[...], dsb, NT)) * slope[:, 0:STATE]
    bcg[:, STATE:] = bc_part[:, STATE:] * slope[:, STATE:]
    bcg.flush()
    edge[:, inner:] = bcg[0:EDGE, :]
    edge.flush()
    onehot = head_onehot(heads, inner, 1)
    kst = head_sums(x * dxst, onehot)
    carry = jnp.sum(sin[...].astype(F32) * st_s[...], axis=0, keepdims=True)
    stack = jnp.concatenate([carry, skp[...], jnp.zeros((6, inner), F32)], axis=0)
    sums = head_sums(stack, onehot)
    dec = sums[0:1, :] * jnp.exp(tot)
    upper = (col_ids(length, length) >= row_ids(length, length)).astype(F32)
    below = (col_ids(length, length) < row_ids(length, length)).astype(F32)
    q = (
        dot(upper, diff[...], precision=HIGHEST)
        + dot(below, kst, precision=HIGHEST)
        + dec
    )
    rate = -jnp.exp(lrate[...])
    sg = sigmoid(upre[...])
    step = rate * q * sg + (kloc_i[...] + kst) * (sg / jnp.maximum(dt, 1e-37))
    dstep[...] = step
    smalls[...] = jnp.zeros(smalls.shape, F32)
    smalls[0:1, 0:heads] = jnp.sum(step, axis=0, keepdims=True)
    smalls[1:2, 0:heads] = jnp.sum(dt * q, axis=0, keepdims=True) * rate
    smalls[2:3, 0:heads] = sums[1:2, :]


def tap_sums(grad, pad, taps):
    length = grad.shape[0]
    for k in range(CONV):
        taps[k : k + 1, :] = jnp.sum(
            grad * pad[EDGE - 3 + k : EDGE - 3 + k + length, :], axis=0, keepdims=True
        )
    taps[CONV : CONV + 1, :] = jnp.sum(grad, axis=0, keepdims=True)
    taps[CONV + 1 :, :] = jnp.zeros((8 - CONV - 1, grad.shape[1]), F32)


def xback_kernel(nxt, xcg, cxw, xpad, xb_a, xb_b, xb, taps, wide):
    length, inner = xcg.shape
    wide[0:length, :] = xcg[...]
    wide[length:, :] = nxt[:, 0:inner]
    grad = xcg[...]
    back = cxw[3:4, :] * grad
    for k in range(CONV - 1):
        back = back + cxw[k : k + 1, :] * wide[3 - k : 3 - k + length, :]
    rounded = back.astype(BF16)
    mid = inner // 2
    xb_a[...] = rounded[:, :mid].astype(F32)
    xb_b[...] = rounded[:, mid:].astype(F32)
    xb[...] = rounded
    for item in (xb_a, xb_b, xb):
        item.flush()
    tap_sums(grad, xpad, taps)


def product_kernel(left, recv_la, recv_lb, right, recv_ra, recv_rb, send_a, send_b, far, near):
    quarter = left.shape[0] // 4
    eighth = quarter // 2
    mid = right.shape[1] // 2
    for which, recv_l, recv_r, send in ((0, recv_la, recv_ra, send_a), (1, recv_lb, recv_rb, send_b)):
        cols = slice(which * mid, which * mid + mid)
        if which == 0:
            rows = left[0 : 2 * quarter, :]
        else:
            rows = jnp.concatenate([left[0:quarter, :], left[2 * quarter : 3 * quarter, :]], axis=0)
        lhs = jnp.concatenate([rows, recv_l[...].astype(BF16)], axis=1)
        rhs = jnp.concatenate([right[:, cols], recv_r[...].astype(BF16)], axis=0)
        send[...] = dot(lhs[quarter:], rhs)
        send.flush()
        kept = dot(lhs[:quarter], rhs)
        near[:, cols] = kept[:eighth]
        far[:, cols] = kept[eighth:]


def in_kernel(
    mine, other, edge_mine, edge_other, cbw, bcpad, first, dstep, wdt, wbc, normed, gg, xb, wz, wx,
    out, bcgrad, dtg, taps, wide, full,
):
    length = mine.shape[0]
    inner = gg.shape[1]
    grad = mine[...] + other[...]
    wide[0:length, :] = grad
    wide[length:, :] = edge_mine[:, inner:] + edge_other[:, inner:]
    back = cbw[3:4, :] * grad
    for k in range(CONV - 1):
        back = back + cbw[k : k + 1, :] * wide[3 - k : 3 - k + length, :]
    bcb = back.astype(BF16)
    step = dstep[...].astype(BF16)
    total = dot(step, wdt[...]) + first[...] * dot(bcb, wbc[...], NT)
    total = total + dot(xb[...], wx[...], NT)
    out[...] = total + dot(gg[...], wz[...], NT)
    out.flush()
    nb = normed[...]
    full[...] = dot(nb, bcb, TN)
    own = lax.axis_index("head") == 0
    rows = full.shape[0] // bcgrad.shape[0]
    for c in range(bcgrad.shape[0]):
        top = full[c * rows : c * rows + rows // 2, :]
        low = full[c * rows + rows // 2 : (c + 1) * rows, :]
        bcgrad[c] = jnp.where(own, top, low)
    bcgrad.flush()
    dtg[...] = dot(step, nb, TN)
    tap_sums(grad, bcpad, taps)


def final_kernel(mine, other, hid, inv, gain, og, grad_in, gain_grad):
    grad = mine[...] + other[...]
    scale = inv[...]
    hat = hid[...] * scale
    gain_grad[...] = jnp.sum(grad * hat, axis=0, keepdims=True)
    hat_in = grad * gain[...]
    grad_in[...] = og[...] + scale * (hat_in - hat * jnp.mean(hat_in * hat, axis=-1, keepdims=True))


def out_kernel(gn, wout, out):
    out[...] = dot(gn[...], wout[...])


def partner(value, bit):
    peers = lax.axis_size("seq")
    return lax.ppermute(value, "seq", [(i, i ^ bit) for i in range(peers)])


def shifted(value, by):
    peers = lax.axis_size("seq")
    return lax.ppermute(value, "seq", [(i, i + by) for i in range(peers) if 0 <= i + by < peers])


def other_head(value):
    return lax.ppermute(value, "head", [(0, 1), (1, 0)])


def exchange(value):
    return lax.all_to_all(value, "seq", 0, 0, tiled=True)


def after(values, *others):
    return lax.optimization_barrier((values, others))[0]


def weight_start(right_a, right_b):
    return partner(right_a, 1), partner(right_b, 2)


def weight_product(left, right, recv):
    full, recv_la, recv_lb = left
    rows = full.shape[0]
    cols = right.shape[1]
    return call(
        product_kernel,
        [f32(rows // 4, cols // 2)] * 2 + [f32(rows // 8, cols)] * 2,
        full, recv_la, recv_lb, right, *recv,
        name="product", flops=4 * rows * cols * right.shape[0],
    )


def weight_second(send_a, send_b):
    return partner(send_a, 2), partner(send_b, 1)


def weight_third(far, near, got):
    got_a, got_b = got
    half = far.shape[0]
    far = far + jnp.concatenate([got_a[half:], got_b[half:]], axis=1)
    near = near + jnp.concatenate([got_a[:half], got_b[:half]], axis=1)
    return far, near


def weight_step(near, got):
    half = near.shape[0] // 2
    return near[half:] + got[half:], near[:half] + got[:half]


def weight_rest(far, near, bit):
    while 2 * bit < lax.axis_size("seq"):
        far, near = weight_step(near, partner(far, bit))
        bit *= 2
    return near + partner(far, bit)


def body(
    hidden_in, norm_gain, proj_z, proj_x, proj_bc, proj_dt, conv_x_weight, conv_x_bias, conv_bc_weight,
    conv_bc_bias, step_bias, log_rate, skip_gain, gate_gain, proj_out, out_grad,
):
    batch, length, width = hidden_in.shape
    heads = step_bias.shape[0]
    inner = proj_z.shape[1]
    n = lax.axis_size("seq")
    place = lax.axis_index("seq")
    side = lax.axis_index("head")
    bits = n.bit_length() - 1
    hid = hidden_in.reshape(length, width)
    og = out_grad.reshape(length, width)
    gain = norm_gain.reshape(1, width)
    ggain = gate_gain.reshape(1, inner)
    sbias = step_bias.reshape(1, heads)
    lrate = log_rate.reshape(1, heads)
    skip = skip_gain.reshape(1, heads)
    wdt = proj_dt.T
    tiles = inner // LANES
    chunk = (STATE // n) * tiles

    edge = shifted(hid[length - EDGE :], 1)
    normed, inv, nfull, nsend_a, nsend_b, gfull, gsend_a, gsend_b = call(
        functools.partial(left_kernel, bits),
        [bf16(length, width), f32(length, 1)]
        + [bf16(width, length), f32(width // 2, length), f32(width // 2, length)] * 2,
        hid, gain, og,
        scratch=[pltpu.VMEM((width, length), F32)] * 2, name="left",
    )
    edge, normed = lax.optimization_barrier((edge, normed))
    nleft = (nfull, partner(nsend_a, 1), partner(nsend_b, 2))
    gleft = (gfull, partner(gsend_a, 1), partner(gsend_b, 2))

    xpad, xconv, xact, bcpad, bcconv, bcact, upre, dts, cums, cumst, dtst, sloc, xw = call(
        front_kernel,
        [
            f32(length + EDGE, inner), f32(length, inner), bf16(length, inner),
            f32(length + EDGE, 2 * STATE), f32(length, 2 * STATE), bf16(length, 2 * STATE),
            f32(length, heads), f32(length, heads), f32(length, heads), f32(heads, length), f32(heads, length),
            f32(n, chunk + tiles, LANES), bf16(length, inner),
        ],
        normed, edge, gain, wdt, sbias, lrate, proj_bc, conv_bc_weight, conv_bc_bias.reshape(1, 2 * STATE),
        conv_x_weight, conv_x_bias.reshape(1, inner), proj_x,
        scratch=[pltpu.VMEM((length + EDGE, width), F32), pltpu.VMEM((STATE, inner), F32)], name="front",
        flops=2 * length * width * (inner + 2 * STATE),
    )
    parts, nleft, gleft = lax.optimization_barrier((exchange(sloc), nleft, gleft))
    scanned, decays = call(scan_kernel, [f32(n, chunk, LANES), f32(n, tiles, LANES)], parts, name="scan")
    gate_pre, ngrad, yloc, mats, decs = call(
        local_kernel,
        [f32(length, inner)] * 3 + [bf16(heads, length, length)] * 2,
        cums, cumst, dtst, bcact, xact, normed, proj_z, og, proj_out,
        name="local", flops=6 * length * width * inner,
    )
    state = pltpu.VMEM((STATE, inner), F32)
    got_states = exchange(scanned)
    sums, yns, sin = call(
        gate_kernel, [f32(length, LANES), f32(length, inner), bf16(STATE, inner)],
        cums, skip, ggain, got_states, bcact, xact, yloc, gate_pre, ngrad, scratch=[state], name="gate",
    )
    half = inner // 2
    sums_other = other_head(sums)
    dsin, dyc, ygrad = call(
        turn_kernel, [f32(n, chunk, LANES), bf16(length, inner), f32(length, inner)],
        sums, sums_other, cums, skip, ggain, bcact, xact, yns, gate_pre, ngrad, scratch=[state], name="turn",
    )
    dparts = exchange(dsin)
    gn, gn_a, gn_b, gg, gg_a, gg_b, ggg, skp = call(
        turn_rest_kernel,
        [bf16(length, inner), f32(length, half), f32(length, half)] * 2 + [f32(1, inner)] * 2,
        sums, sums_other, skip, ggain, xact, yns, gate_pre, ngrad, ygrad, name="turnrest",
    )
    bc_part, diff, kloc, dxloc = call(
        back_kernel,
        [f32(length, 2 * STATE), f32(length, heads), f32(length, heads), f32(length, inner)],
        xact, ygrad, mats, decs, bcact, dyc, sin, yns, name="back", flops=6 * length * length * inner,
    )
    (out_part,) = call(out_kernel, [f32(length, width)], gn, proj_out, name="out", flops=2 * length * width * inner)
    recv_o = weight_start(gn_a, gn_b)
    hidden_out = hid + (out_part + other_head(out_part))
    dparts, hidden_out, dxloc, recv_o = lax.optimization_barrier((dparts, hidden_out, dxloc, recv_o))
    (dscanned,) = call(scan_back_kernel, [f32(n, chunk, LANES)], dparts, decays, name="scanback")
    ds = exchange(dscanned)
    osend_a, osend_b, ofar, onear = weight_product(gleft, gn, after(recv_o, dscanned))
    got_o = weight_second(osend_a, osend_b)
    recv_z = weight_start(*after((gg_a, gg_b), osend_a))
    ds = after(ds, osend_a)

    xcg, bcg, edge_grad, dstep, smalls = call(
        end_kernel,
        [f32(length, inner), f32(length, 2 * STATE), f32(EDGE, inner + 2 * STATE), f32(length, heads), f32(8, LANES)],
        ds, bcact, cums, dts, skip, xw, xact, dxloc, ygrad, xconv, bc_part, bcconv, sin, diff, kloc, upre, lrate, skp,
        scratch=[state], name="end",
    )
    edge_next = shifted(edge_grad, -1)
    ofar, onear = weight_third(ofar, onear, after(got_o, edge_grad))
    got_o = partner(ofar, 4)
    xb_a, xb_b, xb, xtaps = call(
        xback_kernel,
        [f32(length, half), f32(length, half), bf16(length, inner), f32(8, inner)],
        edge_next, xcg, conv_x_weight, xpad,
        scratch=[pltpu.VMEM((length + EDGE, inner), F32)], name="xback",
    )
    recv_x = weight_start(xb_a, xb_b)
    zsend_a, zsend_b, zfar, znear = weight_product(nleft, gg, after(recv_z, edge_grad))
    got_z = weight_second(zsend_a, zsend_b)
    ofar, onear = weight_step(onear, after(got_o, xb))
    grad_out_t = weight_rest(ofar, onear, 8)
    first = (side == 0).astype(F32).reshape(1, 1)
    in_part, bcgrad, dtg, bctaps = call(
        in_kernel,
        [f32(length, width), f32(n, width // n // 2, 2 * STATE), f32(heads, width), f32(8, 2 * STATE)],
        after(bcg, ofar), other_head(bcg), edge_next, other_head(edge_next), conv_bc_weight, bcpad, first, dstep, wdt,
        proj_bc, normed, gg, xb, proj_z, proj_x,
        scratch=[pltpu.VMEM((length + EDGE, 2 * STATE), F32), pltpu.VMEM((width, 2 * STATE), F32)],
        name="in", flops=4 * length * width * inner,
    )
    zfar, znear = weight_third(zfar, znear, after(got_z, in_part))
    got_z = partner(zfar, 4)
    xsend_a, xsend_b, xfar, xnear = weight_product(nleft, xb, after(recv_x, zfar))
    got_x = weight_second(xsend_a, xsend_b)
    grad_in, gain_grad = call(
        final_kernel, [f32(length, width), f32(1, width)],
        in_part, other_head(in_part), after(hid, xsend_a, grad_out_t), inv, gain, og,
        name="final",
    )
    zfar, znear = weight_step(znear, after(got_z, gain_grad))

    rows = width // n
    dt_rows = jnp.transpose(dtg.reshape(heads, n, rows), (1, 0, 2)).reshape(n, heads * rows)
    pack = jnp.concatenate(
        [
            gain_grad.reshape(-1), xtaps[: CONV + 1].reshape(-1), bctaps[: CONV + 1].reshape(-1),
            ggg.reshape(-1), smalls[:3].reshape(-1),
        ]
    )
    size = -(-pack.shape[0] // (n * LANES)) * LANES
    pack = jnp.pad(pack, (0, n * size - pack.shape[0])).reshape(n, size)
    small = jnp.concatenate([dt_rows, pack], axis=1)
    wide = 2 * STATE
    lines = -(-small.shape[1] // wide)
    small = jnp.pad(small, ((0, 0), (0, lines * wide - small.shape[1]))).reshape(n, lines, wide)
    grad_z = weight_rest(zfar, znear, 8)
    reduced = jnp.sum(exchange(jnp.concatenate([bcgrad, after(small, zfar)], axis=1)), axis=0)
    xfar, xnear = weight_third(xfar, xnear, after(got_x, zfar, small))
    got_x = partner(xfar, 4)
    reduced = after(reduced, xfar)
    grad_bc = reduced[: rows // 2]
    reduced = reduced[rows // 2 :].reshape(-1)
    grad_dt = jnp.transpose(reduced[: heads * rows].reshape(heads, rows))
    spreadout = jnp.broadcast_to(
        reduced[heads * rows : heads * rows + size].reshape(1, 1, size), (n, 1, size)
    )
    every = exchange(spreadout).reshape(-1)

    xfar, xnear = weight_step(xnear, after(got_x, grad_z))
    grad_x = weight_rest(xfar, xnear, 8)
    pieces = []
    at = 0
    for count in (width, CONV * inner, inner, CONV * 2 * STATE, 2 * STATE, inner, LANES, LANES, LANES):
        pieces.append(every[at : at + count])
        at += count
    g_norm, g_xw, g_xb, g_bw, g_bb, g_gate, g_step, g_rate, g_skip = pieces
    return (
        hidden_out.reshape(batch, length, width),
        grad_in.reshape(batch, length, width),
        g_norm,
        grad_z,
        grad_x,
        grad_bc,
        grad_dt,
        g_xw.reshape(CONV, inner),
        g_xb,
        g_bw.reshape(CONV, 2 * STATE),
        g_bb,
        g_step[:heads],
        g_rate[:heads],
        g_skip[:heads],
        g_gate,
        grad_out_t.T,
    )


def solution(mesh):
    placed = (
        P(None, "seq", None),
        P(),
        P(None, "head"),
        P(None, "head"),
        P(),
        P(None, "head"),
        P(None, "head"),
        P("head"),
        P(),
        P(),
        P("head"),
        P("head"),
        P("head"),
        P("head"),
        P("head", None),
        P(None, "seq", None),
    )
    return jax.shard_map(
        body,
        mesh=mesh,
        in_specs=placed,
        out_specs=(
            P(None, "seq", None),
            P(None, "seq", None),
            P(),
            P("seq", "head"),
            P("seq", "head"),
            P(("seq", "head"), None),
            P("seq", "head"),
            P(None, "head"),
            P("head"),
            P(),
            P(),
            P("head"),
            P("head"),
            P("head"),
            P("head"),
            P("head", "seq"),
        ),
        check_vma=False,
    )
```

time: 252 us -> 239 us (0.948)
  blocking collectives: 30.9 us -> 0 us
  waiting for transfers between devices: 48.4 us -> 71.8 us
  Pallas kernels: 63.3 us -> 58 us
  starting transfers between devices: 67.7 us -> 72.6 us
  local copies, waits for them, and re-layouts: 24.2 us -> 19.6 us
    all_to_all x2 -> x0, blocking collectives: 30.9 us -> none  [exchange(): return lax.all_to_all(value, 'seq', 0, 0, tiled=True)]
    ppermute x22, waiting for transfers between devices: 25 us -> 51.5 us  [partner(): return lax.ppermute(value, 'seq', [(i, i ^ bit) for i in range(peers)])]
    pallas_call x18 -> x17, Pallas kernels: 63.3 us -> 58 us  [call(): pl.pallas_call(kernel, out_shape=tuple(outs), in_specs=[anywhere] * ins,...]
    all_to_all x6, starting transfers between devices: 26.9 us -> 32.1 us  [exchange(): return lax.all_to_all(value, 'seq', 0, 0, tiled=True)]
    add x8 -> x13, other arithmetic: 7.93 us -> 13.2 us  [the longest x3 5.16 us: weight_rest(): return near + partner(far, bit)]
    all_to_all x6, waiting for transfers between devices: 22 us -> 18.5 us  [exchange(): return lax.all_to_all(value, 'seq', 0, 0, tiled=True)]
    unnamed x63 -> x58, local copies, waits for them, and re-layouts: 9.28 us -> 7.48 us
    ppermute x3 -> x2, starting transfers between devices: 7.6 us -> 6.14 us  [shifted(): lax.ppermute(value, 'seq', [(i, i + by) for i in range(peers) if 0 <= i +...]
  transfers between devices with their start and end apart: 35 -> 35, of which waited for: 11 -> 18; matrix products, arithmetic and copies ran while one was open for 12% -> 9% of each run, Pallas kernels for 19% -> 18%
where the time goes in v2:
time: 239 us; the launch traced here: 237 us
  starting transfers between devices  72.6 us (30%)
  waiting for transfers between devices  71.8 us (30%)
  Pallas kernels  58 us (24%)
  local copies, waits for them, and re-layouts  19.6 us (8%)
  other arithmetic  14.2 us (6%)
    pallas_call x17, Pallas kernels, call(): pl.pallas_call(kernel, out_shape=tuple(outs), in_specs=[anywhere] * ins,...  58 us
    ppermute x22, waiting for transfers between devices, partner(): return lax.ppermute(value, 'seq', [(i, i ^ bit) for i in range(peers)])  51.5 us
    ppermute x22, starting transfers between devices, partner(): return lax.ppermute(value, 'seq', [(i, i ^ bit) for i in range(peers)])  33.8 us
    all_to_all x6, starting transfers between devices, exchange(): return lax.all_to_all(value, 'seq', 0, 0, tiled=True)  32.1 us
    all_to_all x6, waiting for transfers between devices, exchange(): return lax.all_to_all(value, 'seq', 0, 0, tiled=True)  18.5 us
    unnamed x58, local copies, waits for them, and re-layouts  7.48 us
    ppermute x2, starting transfers between devices, shifted(): lax.ppermute(value, 'seq', [(i, i + by) for i in range(peers) if 0 <= i +...  6.14 us
    add x3, other arithmetic, weight_rest(): return near + partner(far, bit)  5.16 us
  transfers between devices with their start and end apart: 35, of which 18 were waited for; matrix products, arithmetic and copies ran while one was open for 9% of the time, Pallas kernels for 18%

profile of v2, /device:TPU:0, one launch (start us, length us, event | category | flops | bytes accessed | tf_op | source)
XLA Modules:
  0.0 237.4 jit_solution(1573261833475407612)
XLA Ops:
  1.4 4.9 %collective-permute-start = (f32[8,1024]{1,0:T(8,128)S(1)}, f32[8,1024]{1,0:T(8,128)S(1)}, u32[]{:S(2)}, u32[]{:S(2)}) collective-permute-start(f32[8,1024]{1,0:T(8,128)S(1)} %slice_bitcast_fusion), channel_id=1, source_target_pairs={{0,2},{2,4},{4,6},{6,8},{8,10},{10,12},{12,14},{14,16},{16,18},{18... | collective-permute-start | bytes 98312 | tf_op jit(solution)/shard_map/ppermute | solution.py:554
  6.3 2.7 %left.1 = (bf16[128,1024]{1,0:T(8,128)(2,1)}, f32[128,1]{1,0:T(8,128)}, bf16[1024,128]{1,0:T(8,128)(2,1)}, f32[512,128]{1,0:T(8,128)}, f32[512,128]{1,0:T(8,128)...) custom-call(f32[128,1024]{1,0:T(8,128)} %bitcast.28, f32[1,1024]{1,0:T(1,128)} %bitcast.44, ...), custom_call_target="tpu_custom_call" | custom-call | bytes 2888192 | tf_op jit(solution)/shard_map/left/pallas_call | solution.py:89
  9.6 5.4 %front.1 = (f32[136,1024]{1,0:T(8,128)}, f32[128,1024]{1,0:T(8,128)}, bf16[128,1024]{1,0:T(8,128)(2,1)}, f32[136,256]{1,0:T(8,128)}, f32[128,256]{1,0:T(8,128)},...) custom-call(bf16[128,1024]{1,0:T(8,128)(2,1)} %get-tuple-element.126, ...), custom_call_target="tpu_custom_call" | custom-call | flops 335544320 | bytes 5551232 | tf_op jit(solution)/shard_map/front/pallas_call | solution.py:89
  15.0 6.6 %all-to-all-start = ((f32[16,72,128]{2,1,0:T(8,128)}), f32[16,72,128]{2,1,0:T(8,128)S(1)}, u32[]{:S(2)}, u32[]{:S(2)}) async-start(f32[16,72,128]{2,1,0:T(8,128)} %get-tuple-element.129), calls=%async_computation | async-start | bytes 1179648 | tf_op jit(solution)/shard_map/all_to_all | solution.py:562
  25.7 11.3 %collective-permute-done.1.refs_1_ = f32[512,128]{1,0:T(8,128)S(1)} collective-permute-done((f32[512,128]{1,0:T(8,128)}, f32[512,128]{1,0:T(8,128)S(1)}, u32[]{:S(2)}, u32[]{:S(2)}) %collective-permute-start.1) | collective-permute-done | bytes 262176 | tf_op jit(solution)/shard_map/ppermute | solution.py:549
  37.0 3.5 %collective-permute-done.3.refs_1_ = f32[512,128]{1,0:T(8,128)S(1)} collective-permute-done((f32[512,128]{1,0:T(8,128)}, f32[512,128]{1,0:T(8,128)S(1)}, u32[]{:S(2)}, u32[]{:S(2)}) %collective-permute-start.3) | collective-permute-done | bytes 262176 | tf_op jit(solution)/shard_map/ppermute | solution.py:549
  43.9 5.1 %all-to-all-start.1 = ((f32[16,64,128]{2,1,0:T(8,128)}), f32[16,64,128]{2,1,0:T(8,128)S(1)}, u32[]{:S(2)}, u32[]{:S(2)}) async-start(f32[16,64,128]{2,1,0:T(8,128)} %get-tuple-element.137), calls=%async_computation.1 | async-start | bytes 1048576 | tf_op jit(solution)/shard_map/all_to_all | solution.py:562
  49.0 4.5 %local.1 = (f32[128,1024]{1,0:T(8,128)}, f32[128,1024]{1,0:T(8,128)}, f32[128,1024]{1,0:T(8,128)}, bf16[16,128,128]{2,1,0:T(8,128)(2,1)}, bf16[16,128,128]{2,1,0:T(8,128)(2,1)}) custom-call(f32[128,16]{1,0:T(8,128)} %get-tuple-element.128.refs_0_.refs_2_, f32[16,128]{1,0:T(8,128)} %get-tuple-element.140.refs_1_, f32[16,128]{1,0:T(8,128)} %get-tuple-element.141.refs_2_, ...), custom_call_target="tpu_custom_call" | custom-call | flops 805306368 | bytes 7954432 | tf_op jit(solution)/shard_map/local/pallas_call | solution.py:89
  53.5 10.0 %all-to-all-done.1.refs_3_ = f32[16,64,128]{2,1,0:T(8,128)S(1)} async-done(((f32[16,64,128]{2,1,0:T(8,128)}), f32[16,64,128]{2,1,0:T(8,128)S(1)}, u32[]{:S(2)}, u32[]{:S(2)}) %all-to-all-start.1) | async-done | bytes 524320 | tf_op jit(solution)/shard_map/all_to_all | solution.py:562
  64.3 3.2 %gate.1 = (f32[128,128]{1,0:T(8,128)}, f32[128,1024]{1,0:T(8,128)}, bf16[128,1024]{1,0:T(8,128)(2,1)}) custom-call(f32[128,16]{1,0:T(8,128)} %get-tuple-element.128.refs_0_.refs_2_, f32[1,16]{1,0:T(1,128)} %bitcast.50, f32[1,1024]{1,0:T(1,128)} %bitcast.41, f32[16,64,128]{2,1,0:T(8,128)} %copy-done.4, ...), custom_call_target="tpu_custom_call" | custom-call | bytes 3289152 | tf_op jit(solution)/shard_map/gate/pallas_call | solution.py:89
  69.7 3.4 %turn.1 = (f32[16,64,128]{2,1,0:T(8,128)}, bf16[128,1024]{1,0:T(8,128)(2,1)}, f32[128,1024]{1,0:T(8,128)}) custom-call(f32[128,128]{1,0:T(8,128)} %get-tuple-element.145.refs_0_, f32[128,128]{1,0:T(8,128)} %copy-done.13, f32[128,16]{1,0:T(8,128)} %get-tuple-element.128.refs_0_.refs_2_, f32[1,16]{1,0:T(1,128)} %bitcast.51, f32[1,1024]{1,0:T(1,128)} %bitcast.42, ...), custom_call_target="tpu_custom_call" | custom-call | bytes 3354688 | tf_op jit(solution)/shard_map/turn/pallas_call | solution.py:89
  73.1 4.0 %all-to-all-start.2 = ((f32[16,64,128]{2,1,0:T(8,128)}), f32[16,64,128]{2,1,0:T(8,128)S(1)}, u32[]{:S(2)}, u32[]{:S(2)}) async-start(f32[16,64,128]{2,1,0:T(8,128)} %get-tuple-element.147), calls=%async_computation.2 | async-start | bytes 1048576 | tf_op jit(solution)/shard_map/all_to_all | solution.py:562
  77.1 3.3 %turnrest.1 = (bf16[128,1024]{1,0:T(8,128)(2,1)}, f32[128,512]{1,0:T(8,128)}, f32[128,512]{1,0:T(8,128)}, bf16[128,1024]{1,0:T(8,128)(2,1)}, f32[128,512]{1,0:T(...) custom-call(f32[128,128]{1,0:T(8,128)} %get-tuple-element.145.refs_0_, f32[128,128]{1,0:T(8,128)} %copy-done.13, ...), custom_call_target="tpu_custom_call" | custom-call | bytes 4075584 | tf_op jit(solution)/shard_map/turnrest/pallas_call | solution.py:89
  80.4 3.0 %out.1 = f32[128,1024]{1,0:T(8,128)} custom-call(bf16[128,1024]{1,0:T(8,128)(2,1)} %get-tuple-element.149.refs_0_.refs_3_, bf16[1024,1024]{1,0:T(8,128)(2,1)} %refs_1_.1), custom_call_target="tpu_custom_call" | custom-call | flops 268435456 | bytes 2883584 | tf_op jit(solution)/shard_map/out/pallas_call | solution.py:89
  86.9 3.9 %back.1 = (f32[128,256]{1,0:T(8,128)}, f32[128,16]{1,0:T(8,128)}, f32[128,16]{1,0:T(8,128)}, f32[128,1024]{1,0:T(8,128)}) custom-call(bf16[128,1024]{1,0:T(8,128)(2,1)} %get-tuple-element.139.refs_4_.refs_5_.refs_6_.refs_0_, f32[128,1024]{1,0:T(8,128)} %get-tuple-element.148.refs_8_.refs_1_, bf16[16,128,128]{2,1,0:T(8,128)(2,1)} %get-tuple-element.150.refs_2_, ...), custom_call_target="tpu_custom_call" | custom-call | flops 100663296 | bytes 3620864 | tf_op jit(solution)/shard_map/back/pallas_call | solution.py:89
  98.1 5.5 %all-to-all-start.3 = ((f32[16,64,128]{2,1,0:T(8,128)}), f32[16,64,128]{2,1,0:T(8,128)S(1)}, u32[]{:S(2)}, u32[]{:S(2)}) async-start(f32[16,64,128]{2,1,0:T(8,128)} %scanback.1), calls=%async_computation.3 | async-start | bytes 1048576 | tf_op jit(solution)/shard_map/all_to_all | solution.py:562
  103.6 3.1 %product.3 = (f32[256,512]{1,0:T(8,128)}, f32[256,512]{1,0:T(8,128)}, f32[128,1024]{1,0:T(8,128)}, f32[128,1024]{1,0:T(8,128)}) custom-call(bf16[1024,128]{1,0:T(8,128)(2,1)} %get-tuple-element.160.refs_0_, f32[512,128]{1,0:T(8,128)} %copy-done.25, f32[512,128]{1,0:T(8,128)} %copy-done.26, bf16[128,1024]{1,0:T(8,128)(2,1)} %get-tuple-element.149.refs_0_.refs_3_, ...), custom_call_target="tpu_custom_call" | custom-call | flops 536870912 | bytes 3670016 | tf_op jit(solution)/shard_map/product/pallas_call | solution.py:89
  110.9 7.8 %all-to-all-done.3.refs_0_ = f32[16,64,128]{2,1,0:T(8,128)S(1)} async-done(((f32[16,64,128]{2,1,0:T(8,128)}), f32[16,64,128]{2,1,0:T(8,128)S(1)}, u32[]{:S(2)}, u32[]{:S(2)}) %all-to-all-start.3) | async-done | bytes 524320 | tf_op jit(solution)/shard_map/all_to_all | solution.py:562
  119.4 4.4 %end.1 = (f32[128,1024]{1,0:T(8,128)}, f32[128,256]{1,0:T(8,128)}, f32[8,1280]{1,0:T(8,128)}, f32[128,16]{1,0:T(8,128)}, f32[8,128]{1,0:T(8,128)}) custom-call(f32[16,64,128]{2,1,0:T(8,128)} %copy-done.2, bf16[128,256]{1,0:T(8,128)(2,1)} %get-tuple-element.138.refs_3_.refs_4_.refs_5_.refs_1_, f32[128,16]{1,0:T(8,128)} %get-tuple-element.128.refs_0_.refs_2_, ...), custom_call_target="tpu_custom_call" | custom-call | bytes 3965056 | tf_op jit(solution)/shard_map/end/pallas_call | solution.py:89
  131.6 3.1 %product.4 = (f32[256,512]{1,0:T(8,128)}, f32[256,512]{1,0:T(8,128)}, f32[128,1024]{1,0:T(8,128)}, f32[128,1024]{1,0:T(8,128)}) custom-call(bf16[1024,128]{1,0:T(8,128)(2,1)} %get-tuple-element.195.refs_0_, f32[512,128]{1,0:T(8,128)} %copy-done.22, f32[512,128]{1,0:T(8,128)} %copy-done.23, bf16[128,1024]{1,0:T(8,128)(2,1)} %get-tuple-element.193.refs_11_.refs_3_, ...), custom_call_target="tpu_custom_call" | custom-call | flops 536870912 | bytes 3670016 | tf_op jit(solution)/shard_map/product/pallas_call | solution.py:89
  134.6 2.9 %collective-permute-start.20 = (f32[256,512]{1,0:T(8,128)}, f32[256,512]{1,0:T(8,128)}, u32[]{:S(2)}, u32[]{:S(2)}) collective-permute-start(f32[256,512]{1,0:T(8,128)} %get-tuple-element.207), channel_id=1, source_target_pairs={{0,4},{2,6},{4,0},{6,2},{8,12},{10,14},{12,8},{14,10},{16,20},{18,... | collective-permute-start | bytes 1572872 | tf_op jit(solution)/shard_map/ppermute | solution.py:549
  145.2 4.1 %collective-permute-start.17 = (f32[128,512]{1,0:T(8,128)}, f32[128,512]{1,0:T(8,128)}, u32[]{:S(2)}, u32[]{:S(2)}) collective-permute-start(f32[128,512]{1,0:T(8,128)} %get-tuple-element.199), channel_id=1, source_target_pairs={{0,4},{2,6},{4,0},{6,2},{8,12},{10,14},{12,8},{14,10},{16,20},{18,... | collective-permute-start | bytes 786440 | tf_op jit(solution)/shard_map/ppermute | solution.py:549
  149.3 3.0 %collective-permute-start.22 = (f32[64,1024]{1,0:T(8,128)S(1)}, f32[64,1024]{1,0:T(8,128)}, u32[]{:S(2)}, u32[]{:S(2)}) collective-permute-start(f32[64,1024]{1,0:T(8,128)S(1)} %slice_add_fusion.5), channel_id=1, source_target_pairs={{0,16},{2,18},{4,20},{6,22},{8,24},{10,26},{12,28},{14,30},{16,0},... | collective-permute-start | bytes 786440 | tf_op jit(solution)/shard_map/ppermute | solution.py:549
  152.3 5.8 %in.1 = (f32[128,1024]{1,0:T(8,128)}, f32[16,32,256]{2,1,0:T(8,128)}, f32[16,1024]{1,0:T(8,128)}, f32[8,256]{1,0:T(8,128)}) custom-call(f32[128,256]{1,0:T(8,128)} %get-tuple-element.190.refs_0_, f32[128,256]{1,0:T(8,128)} %collective-permute-done.13.refs_1_, f32[8,1280]{1,0:T(8,128)} %copy-done.14, f32[8,1280]{1,0:T(8,128)} %copy-done.17, ...), custom_call_target="tpu_custom_call" | custom-call | flops 536870912 | bytes 7155716 | tf_op jit(solution)/shard_map/in/pallas_call | solution.py:89
  161.3 3.1 %product.5 = (f32[256,512]{1,0:T(8,128)}, f32[256,512]{1,0:T(8,128)}, f32[128,1024]{1,0:T(8,128)}, f32[128,1024]{1,0:T(8,128)}) custom-call(bf16[1024,128]{1,0:T(8,128)(2,1)} %get-tuple-element.195.refs_0_, f32[512,128]{1,0:T(8,128)} %copy-done.22, f32[512,128]{1,0:T(8,128)} %copy-done.23, bf16[128,1024]{1,0:T(8,128)(2,1)} %get-tuple-element.188.refs_12_.refs_3_, ...), custom_call_target="tpu_custom_call" | custom-call | flops 536870912 | bytes 3670016 | tf_op jit(solution)/shard_map/product/pallas_call | solution.py:89
  168.3 2.6 %final.1 = (f32[128,1024]{1,0:T(8,128)}, f32[1,1024]{1,0:T(1,128)}) custom-call(f32[128,1024]{1,0:T(8,128)} %get-tuple-element.194.refs_0_, f32[128,1024]{1,0:T(8,128)} %collective-permute-done.15.refs_1_, f32[128,1024]{1,0:T(8,128)} %bitcast.29, f32[128,1]{1,0:T(8,128)} %get-tuple-element.215.refs_3_, f32[1,1024]{1,0:T(1,128)} %bitcast.46, f32[128,1024]{1,0:T(8,128)} %bitcast.32), custom_call_target="tpu_custom_call" | custom-call | bytes 2630144 | tf_op jit(solution)/shard_map/final/pallas_call | solution.py:89
  171.7 4.2 %collective-permute-done.23 = f32[128,1024]{1,0:T(8,128)} collective-permute-done((f32[128,1024]{1,0:T(8,128)}, f32[128,1024]{1,0:T(8,128)}, u32[]{:S(2)}, u32[]{:S(2)}) %collective-permute-start.23) | collective-permute-done | bytes 524320 | tf_op jit(solution)/shard_map/ppermute | solution.py:549
  182.5 4.2 %all-to-all-start.4 = ((f32[16,39,256]{2,1,0:T(8,128)}), f32[16,39,256]{2,1,0:T(8,128)S(1)}, u32[]{:S(2)}, u32[]{:S(2)}) async-start(f32[16,39,256]{2,1,0:T(8,128)} %pad_maximum_fusion), calls=%async_computation.4 | async-start | bytes 1310720 | tf_op jit(solution)/shard_map/all_to_all | solution.py:562
  192.2 21.3 %collective-permute-done.26 = f32[64,1024]{1,0:T(8,128)S(1)} collective-permute-done((f32[64,1024]{1,0:T(8,128)S(1)}, f32[64,1024]{1,0:T(8,128)S(1)}, u32[]{:S(2)}, u32[]{:S(2)}) %collective-permute-start.26) | collective-permute-done | bytes 262176 | tf_op jit(solution)/shard_map/ppermute | solution.py:549
  216.5 3.0 %collective-permute-start.28 = (f32[64,1024]{1,0:T(8,128)S(1)}, f32[64,1024]{1,0:T(8,128)S(1)}, u32[]{:S(2)}, u32[]{:S(2)}) collective-permute-start(f32[64,1024]{1,0:T(8,128)S(1)} %slice_add_fusion), channel_id=1, source_target_pairs={{0,16},{2,18},{4,20},{6,22},{8,24},{10,26},{12,28},{14,30},{16,0},... | collective-permute-start | bytes 786440 | tf_op jit(solution)/shard_map/ppermute | solution.py:549
  220.1 6.8 %all-to-all-start.5 = ((f32[16,1,640]{2,1,0:T(1,128)}), f32[16,1,640]{2,1,0:T(1,128)S(1)}, u32[]{:S(2)}, u32[]{:S(2)}) async-start(f32[16,1,640]{2,1,0:T(1,128)} %broadcast_in_dim.2), calls=%async_computation.5 | async-start | bytes 81920 | tf_op jit(solution)/shard_map/all_to_all | solution.py:562
  226.9 3.7 %collective-permute-done.28 = f32[64,1024]{1,0:T(8,128)S(1)} collective-permute-done((f32[64,1024]{1,0:T(8,128)S(1)}, f32[64,1024]{1,0:T(8,128)S(1)}, u32[]{:S(2)}, u32[]{:S(2)}) %collective-permute-start.28) | collective-permute-done | bytes 262176 | tf_op jit(solution)/shard_map/ppermute | solution.py:549
  (159 shorter events, 72.9 us)
Async XLA Ops:
  1.4 7.5 %collective-permute-start = (f32[8,1024]{1,0:T(8,128)S(1)}, f32[8,1024]{1,0:T(8,128)S(1)}, u32[]{:S(2)}, u32[]{:S(2)}) collective-permute-start(f32[8,1024]{1,0:T(8,128)S(1)} %slice_bitcast_fusion), channel_id=1, source_target_pairs={{0,2},{2,4},{4,6},{6,8},{8,10},{10,12},{12,14},{14,16},{16,18},{18... | collective-permute-start | bytes 98312 | tf_op jit(solution)/shard_map/ppermute | solution.py:554
  15.0 26.0 %all-to-all-start = ((f32[16,72,128]{2,1,0:T(8,128)}), f32[16,72,128]{2,1,0:T(8,128)S(1)}, u32[]{:S(2)}, u32[]{:S(2)}) async-start(f32[16,72,128]{2,1,0:T(8,128)} %get-tuple-element.129), calls=%async_computation | async-start | bytes 1179648 | tf_op jit(solution)/shard_map/all_to_all | solution.py:562
  21.6 15.4 %collective-permute-start.1 = (f32[512,128]{1,0:T(8,128)}, f32[512,128]{1,0:T(8,128)S(1)}, u32[]{:S(2)}, u32[]{:S(2)}) collective-permute-start(f32[512,128]{1,0:T(8,128)} %get-tuple-element.131), channel_id=1, source_target_pairs={{0,2},{2,0},{4,6},{6,4},{8,10},{10,8},{12,14},{14,12},{16,18},{18,... | collective-permute-start | bytes 786440 | tf_op jit(solution)/shard_map/ppermute | solution.py:549
  23.6 13.5 %collective-permute-start.2 = (f32[512,128]{1,0:T(8,128)}, f32[512,128]{1,0:T(8,128)S(1)}, u32[]{:S(2)}, u32[]{:S(2)}) collective-permute-start(f32[512,128]{1,0:T(8,128)} %get-tuple-element.132), channel_id=1, source_target_pairs={{0,4},{2,6},{4,0},{6,2},{8,12},{10,14},{12,8},{14,10},{16,20},{18,... | collective-permute-start | bytes 786440 | tf_op jit(solution)/shard_map/ppermute | solution.py:549
  25.0 15.5 %collective-permute-start.3 = (f32[512,128]{1,0:T(8,128)}, f32[512,128]{1,0:T(8,128)S(1)}, u32[]{:S(2)}, u32[]{:S(2)}) collective-permute-start(f32[512,128]{1,0:T(8,128)} %get-tuple-element.134), channel_id=1, source_target_pairs={{0,2},{2,0},{4,6},{6,4},{8,10},{10,8},{12,14},{14,12},{16,18},{18,... | collective-permute-start | bytes 786440 | tf_op jit(solution)/shard_map/ppermute | solution.py:549
  25.6 15.4 %collective-permute-start.4 = (f32[512,128]{1,0:T(8,128)}, f32[512,128]{1,0:T(8,128)S(1)}, u32[]{:S(2)}, u32[]{:S(2)}) collective-permute-start(f32[512,128]{1,0:T(8,128)} %get-tuple-element.135), channel_id=1, source_target_pairs={{0,4},{2,6},{4,0},{6,2},{8,12},{10,14},{12,8},{14,10},{16,20},{18,... | collective-permute-start | bytes 786440 | tf_op jit(solution)/shard_map/ppermute | solution.py:549
  43.9 19.6 %all-to-all-start.1 = ((f32[16,64,128]{2,1,0:T(8,128)}), f32[16,64,128]{2,1,0:T(8,128)S(1)}, u32[]{:S(2)}, u32[]{:S(2)}) async-start(f32[16,64,128]{2,1,0:T(8,128)} %get-tuple-element.137), calls=%async_computation.1 | async-start | bytes 1048576 | tf_op jit(solution)/shard_map/all_to_all | solution.py:562
  73.1 22.2 %all-to-all-start.2 = ((f32[16,64,128]{2,1,0:T(8,128)}), f32[16,64,128]{2,1,0:T(8,128)S(1)}, u32[]{:S(2)}, u32[]{:S(2)}) async-start(f32[16,64,128]{2,1,0:T(8,128)} %get-tuple-element.147), calls=%async_computation.2 | async-start | bytes 1048576 | tf_op jit(solution)/shard_map/all_to_all | solution.py:562
  83.5 11.2 %collective-permute-start.7 = (f32[128,512]{1,0:T(8,128)}, f32[128,512]{1,0:T(8,128)}, u32[]{:S(2)}, u32[]{:S(2)}) collective-permute-start(f32[128,512]{1,0:T(8,128)} %get-tuple-element.155), channel_id=1, source_target_pairs={{0,2},{2,0},{4,6},{6,4},{8,10},{10,8},{12,14},{14,12},{16,18},{18,... | collective-permute-start | bytes 786440 | tf_op jit(solution)/shard_map/ppermute | solution.py:549
  85.5 9.9 %collective-permute-start.8 = (f32[128,512]{1,0:T(8,128)}, f32[128,512]{1,0:T(8,128)}, u32[]{:S(2)}, u32[]{:S(2)}) collective-permute-start(f32[128,512]{1,0:T(8,128)} %get-tuple-element.156), channel_id=1, source_target_pairs={{0,4},{2,6},{4,0},{6,2},{8,12},{10,14},{12,8},{14,10},{16,20},{18,... | collective-permute-start | bytes 786440 | tf_op jit(solution)/shard_map/ppermute | solution.py:549
  98.1 20.5 %all-to-all-start.3 = ((f32[16,64,128]{2,1,0:T(8,128)}), f32[16,64,128]{2,1,0:T(8,128)S(1)}, u32[]{:S(2)}, u32[]{:S(2)}) async-start(f32[16,64,128]{2,1,0:T(8,128)} %scanback.1), calls=%async_computation.3 | async-start | bytes 1048576 | tf_op jit(solution)/shard_map/all_to_all | solution.py:562
  106.7 18.6 %collective-permute-start.10 = (f32[256,512]{1,0:T(8,128)}, f32[256,512]{1,0:T(8,128)S(1)}, u32[]{:S(2)}, u32[]{:S(2)}) collective-permute-start(f32[256,512]{1,0:T(8,128)} %get-tuple-element.181), channel_id=1, source_target_pairs={{0,2},{2,0},{4,6},{6,4},{8,10},{10,8},{12,14},{14,12},{16,18},{18,... | collective-permute-start | bytes 1572872 | tf_op jit(solution)/shard_map/ppermute | solution.py:549
  108.7 16.8 %collective-permute-start.9 = (f32[256,512]{1,0:T(8,128)}, f32[256,512]{1,0:T(8,128)S(1)}, u32[]{:S(2)}, u32[]{:S(2)}) collective-permute-start(f32[256,512]{1,0:T(8,128)} %get-tuple-element.167), channel_id=1, source_target_pairs={{0,4},{2,6},{4,0},{6,2},{8,12},{10,14},{12,8},{14,10},{16,20},{18,... | collective-permute-start | bytes 1572872 | tf_op jit(solution)/shard_map/ppermute | solution.py:549
  110.2 21.3 %collective-permute-start.18 = (f32[128,512]{1,0:T(8,128)}, f32[128,512]{1,0:T(8,128)}, u32[]{:S(2)}, u32[]{:S(2)}) collective-permute-start(f32[128,512]{1,0:T(8,128)} %get-tuple-element.202), channel_id=1, source_target_pairs={{0,2},{2,0},{4,6},{6,4},{8,10},{10,8},{12,14},{14,12},{16,18},{18,... | collective-permute-start | bytes 786440 | tf_op jit(solution)/shard_map/ppermute | solution.py:549
  110.8 20.8 %collective-permute-start.19 = (f32[128,512]{1,0:T(8,128)S(1)}, f32[128,512]{1,0:T(8,128)}, u32[]{:S(2)}, u32[]{:S(2)}) collective-permute-start(f32[128,512]{1,0:T(8,128)S(1)} %copy-done.24), channel_id=1, source_target_pairs={{0,4},{2,6},{4,0},{6,2},{8,12},{10,14},{12,8},{14,10},{16,20},{18,... | collective-permute-start | bytes 786440 | tf_op jit(solution)/shard_map/ppermute | solution.py:549
  128.3 15.4 %collective-permute-start.11 = (f32[128,1024]{1,0:T(8,128)}, f32[128,1024]{1,0:T(8,128)}, u32[]{:S(2)}, u32[]{:S(2)}) collective-permute-start(f32[128,1024]{1,0:T(8,128)} %maximum_add_fusion.1), channel_id=1, source_target_pairs={{0,8},{2,10},{4,12},{6,14},{8,0},{10,2},{12,4},{14,6},{16,24},{18,... | collective-permute-start | bytes 1572872 | tf_op jit(solution)/shard_map/ppermute | solution.py:549
  130.2 8.4 %collective-permute-start.12 = (f32[8,1280]{1,0:T(8,128)}, f32[8,1280]{1,0:T(8,128)S(1)}, u32[]{:S(2)}, u32[]{:S(2)}) collective-permute-start(f32[8,1280]{1,0:T(8,128)} %get-tuple-element.182), channel_id=1, source_target_pairs={{2,0},{4,2},{6,4},{8,6},{10,8},{12,10},{14,12},{16,14},{18,16},{20... | collective-permute-start | bytes 122888 | tf_op jit(solution)/shard_map/ppermute | solution.py:554
  134.6 23.5 %collective-permute-start.20 = (f32[256,512]{1,0:T(8,128)}, f32[256,512]{1,0:T(8,128)}, u32[]{:S(2)}, u32[]{:S(2)}) collective-permute-start(f32[256,512]{1,0:T(8,128)} %get-tuple-element.207), channel_id=1, source_target_pairs={{0,4},{2,6},{4,0},{6,2},{8,12},{10,14},{12,8},{14,10},{16,20},{18,... | collective-permute-start | bytes 1572872 | tf_op jit(solution)/shard_map/ppermute | solution.py:549
  137.6 20.6 %collective-permute-start.21 = (f32[256,512]{1,0:T(8,128)}, f32[256,512]{1,0:T(8,128)}, u32[]{:S(2)}, u32[]{:S(2)}) collective-permute-start(f32[256,512]{1,0:T(8,128)} %get-tuple-element.208), channel_id=1, source_target_pairs={{0,2},{2,0},{4,6},{6,4},{8,10},{10,8},{12,14},{14,12},{16,18},{18,... | collective-permute-start | bytes 1572872 | tf_op jit(solution)/shard_map/ppermute | solution.py:549
  138.6 10.7 %collective-permute-start.13 = (f32[128,256]{1,0:T(8,128)S(1)}, f32[128,256]{1,0:T(8,128)}, u32[]{:S(2)}, u32[]{:S(2)}) collective-permute-start(f32[128,256]{1,0:T(8,128)S(1)} %copy-done.15), channel_id=1, source_target_pairs={{0,1},{1,0},{2,3},{3,2},{4,5},{5,4},{6,7},{7,6},{8,9},{9,8},{10,11... | collective-permute-start | bytes 393224 | tf_op jit(solution)/shard_map/ppermute | solution.py:558
  141.8 19.5 %collective-permute-start.16 = (f32[128,512]{1,0:T(8,128)}, f32[128,512]{1,0:T(8,128)}, u32[]{:S(2)}, u32[]{:S(2)}) collective-permute-start(f32[128,512]{1,0:T(8,128)} %get-tuple-element.198), channel_id=1, source_target_pairs={{0,2},{2,0},{4,6},{6,4},{8,10},{10,8},{12,14},{14,12},{16,18},{18,... | collective-permute-start | bytes 786440 | tf_op jit(solution)/shard_map/ppermute | solution.py:549
  145.2 16.2 %collective-permute-start.17 = (f32[128,512]{1,0:T(8,128)}, f32[128,512]{1,0:T(8,128)}, u32[]{:S(2)}, u32[]{:S(2)}) collective-permute-start(f32[128,512]{1,0:T(8,128)} %get-tuple-element.199), channel_id=1, source_target_pairs={{0,4},{2,6},{4,0},{6,2},{8,12},{10,14},{12,8},{14,10},{16,20},{18,... | collective-permute-start | bytes 786440 | tf_op jit(solution)/shard_map/ppermute | solution.py:549
  149.3 17.3 %collective-permute-start.22 = (f32[64,1024]{1,0:T(8,128)S(1)}, f32[64,1024]{1,0:T(8,128)}, u32[]{:S(2)}, u32[]{:S(2)}) collective-permute-start(f32[64,1024]{1,0:T(8,128)S(1)} %slice_add_fusion.5), channel_id=1, source_target_pairs={{0,16},{2,18},{4,20},{6,22},{8,24},{10,26},{12,28},{14,30},{16,0},... | collective-permute-start | bytes 786440 | tf_op jit(solution)/shard_map/ppermute | solution.py:549
  158.1 10.2 %collective-permute-start.15 = (f32[128,1024]{1,0:T(8,128)}, f32[128,1024]{1,0:T(8,128)}, u32[]{:S(2)}, u32[]{:S(2)}) collective-permute-start(f32[128,1024]{1,0:T(8,128)} %get-tuple-element.194.refs_0_), channel_id=1, source_target_pairs={{0,1},{1,0},{2,3},{3,2},{4,5},{5,4},{6,7},{7,6},{8,9},{9,8},{10,11... | collective-permute-start | bytes 1572872 | tf_op jit(solution)/shard_map/ppermute | solution.py:558
  161.3 14.6 %collective-permute-start.23 = (f32[128,1024]{1,0:T(8,128)}, f32[128,1024]{1,0:T(8,128)}, u32[]{:S(2)}, u32[]{:S(2)}) collective-permute-start(f32[128,1024]{1,0:T(8,128)} %maximum_add_fusion.2), channel_id=1, source_target_pairs={{0,8},{2,10},{4,12},{6,14},{8,0},{10,2},{12,4},{14,6},{16,24},{18,... | collective-permute-start | bytes 1572872 | tf_op jit(solution)/shard_map/ppermute | solution.py:549
  164.7 14.6 %collective-permute-start.24 = (f32[256,512]{1,0:T(8,128)}, f32[256,512]{1,0:T(8,128)}, u32[]{:S(2)}, u32[]{:S(2)}) collective-permute-start(f32[256,512]{1,0:T(8,128)} %get-tuple-element.213), channel_id=1, source_target_pairs={{0,4},{2,6},{4,0},{6,2},{8,12},{10,14},{12,8},{14,10},{16,20},{18,... | collective-permute-start | bytes 1572872 | tf_op jit(solution)/shard_map/ppermute | solution.py:549
  164.8 14.6 %collective-permute-start.25 = (f32[256,512]{1,0:T(8,128)}, f32[256,512]{1,0:T(8,128)}, u32[]{:S(2)}, u32[]{:S(2)}) collective-permute-start(f32[256,512]{1,0:T(8,128)} %get-tuple-element.228), channel_id=1, source_target_pairs={{0,2},{2,0},{4,6},{6,4},{8,10},{10,8},{12,14},{14,12},{16,18},{18,... | collective-permute-start | bytes 1572872 | tf_op jit(solution)/shard_map/ppermute | solution.py:549
  182.5 36.9 %all-to-all-start.4 = ((f32[16,39,256]{2,1,0:T(8,128)}), f32[16,39,256]{2,1,0:T(8,128)S(1)}, u32[]{:S(2)}, u32[]{:S(2)}) async-start(f32[16,39,256]{2,1,0:T(8,128)} %pad_maximum_fusion), calls=%async_computation.4 | async-start | bytes 1310720 | tf_op jit(solution)/shard_map/all_to_all | solution.py:562
  187.8 27.8 %collective-permute-start.27 = (f32[128,1024]{1,0:T(8,128)S(1)}, f32[128,1024]{1,0:T(8,128)S(1)}, u32[]{:S(2)}, u32[]{:S(2)}) collective-permute-start(f32[128,1024]{1,0:T(8,128)S(1)} %maximum_add_fusion.4), channel_id=1, source_target_pairs={{0,8},{2,10},{4,12},{6,14},{8,0},{10,2},{12,4},{14,6},{16,24},{18,... | collective-permute-start | bytes 1572872 | tf_op jit(solution)/shard_map/ppermute | solution.py:549
  189.8 23.7 %collective-permute-start.26 = (f32[64,1024]{1,0:T(8,128)S(1)}, f32[64,1024]{1,0:T(8,128)S(1)}, u32[]{:S(2)}, u32[]{:S(2)}) collective-permute-start(f32[64,1024]{1,0:T(8,128)S(1)} %slice_add_fusion.3), channel_id=1, source_target_pairs={{0,16},{2,18},{4,20},{6,22},{8,24},{10,26},{12,28},{14,30},{16,0},... | collective-permute-start | bytes 786440 | tf_op jit(solution)/shard_map/ppermute | solution.py:549
  216.5 14.2 %collective-permute-start.28 = (f32[64,1024]{1,0:T(8,128)S(1)}, f32[64,1024]{1,0:T(8,128)S(1)}, u32[]{:S(2)}, u32[]{:S(2)}) collective-permute-start(f32[64,1024]{1,0:T(8,128)S(1)} %slice_add_fusion), channel_id=1, source_target_pairs={{0,16},{2,18},{4,20},{6,22},{8,24},{10,26},{12,28},{14,30},{16,0},... | collective-permute-start | bytes 786440 | tf_op jit(solution)/shard_map/ppermute | solution.py:549
  220.1 14.2 %all-to-all-start.5 = ((f32[16,1,640]{2,1,0:T(1,128)}), f32[16,1,640]{2,1,0:T(1,128)S(1)}, u32[]{:S(2)}, u32[]{:S(2)}) async-start(f32[16,1,640]{2,1,0:T(1,128)} %broadcast_in_dim.2), calls=%async_computation.5 | async-start | bytes 81920 | tf_op jit(solution)/shard_map/all_to_all | solution.py:562
  (30 other events, 266.2 us)
